TPU v7x, 32 devices: a whole 2x2x4 slice. The times are simulated.
32 devices in a mesh: rep: 4 (over z), shard: 8 (over y, x, core).
Axes of the slice: x: 2, y: 2, z: 4, core: 2. Of those that a mesh axis runs over, the one named last changes fastest.
Arguments:
- inputs: bfloat16 [65536, 768], P(('rep', 'shard')), may hold values from -6 to 6
- cotangent: bfloat16 [65536, 768], P(('rep', 'shard')), may hold values from -6 to 6
- picture_ids: int32 [65536], P(('rep', 'shard')), may hold values from 0 to 19, as said below
- picture_lengths: int32 [32, 20], P(('rep', 'shard')), may hold values from 0 to 1024, as said below
- picture_offsets: int32 [32, 20], P(('rep', 'shard')), may hold values from 0 to 2048, as said below
- padding: int32 [65536], P(('rep', 'shard')), may hold values from 0 to 1, as said below
- ln1_gain: bfloat16 [768], P('shard'), may hold values from 0.099609375 to 1.8984375
- ln1_bias: bfloat16 [768], P('shard'), may hold values from -4 to 4
- qkv_weight: bfloat16 [768, 2304], P('shard'), may hold values from -0.21875 to 0.21875
- qkv_bias: bfloat16 [2304], P('shard'), may hold values from -4 to 4
- query_gain: bfloat16 [64], P('shard'), may hold values from 0.099609375 to 1.8984375
- key_gain: bfloat16 [64], P('shard'), may hold values from 0.099609375 to 1.8984375
- out_weight: bfloat16 [768, 768], P('shard'), may hold values from -0.875 to 0.875
- out_bias: bfloat16 [768], P('shard'), may hold values from -4 to 4
- ln2_gain: bfloat16 [768], P('shard'), may hold values from 0.099609375 to 1.8984375
- ln2_bias: bfloat16 [768], P('shard'), may hold values from -4 to 4
- up_weight: bfloat16 [768, 3072], P('shard'), may hold values from -0.21875 to 0.21875
- up_bias: bfloat16 [3072], P('shard'), may hold values from -4 to 4
- down_weight: bfloat16 [3072, 768], P('shard'), may hold values from -0.109375 to 0.109375
- down_bias: bfloat16 [768], P('shard'), may hold values from -4 to 4
Outputs:
- output: bfloat16 [65536, 768], P(('rep', 'shard'))
- input_grad: float32 [65536, 768], P(('rep', 'shard'))
- ln1_gain_grad: float32 [768], P('shard')
- ln1_bias_grad: float32 [768], P('shard')
- qkv_weight_grad: float32 [768, 2304], P('shard')
- qkv_bias_grad: float32 [2304], P('shard')
- query_gain_grad: float32 [64], P('shard')
- key_gain_grad: float32 [64], P('shard')
- out_weight_grad: float32 [768, 768], P('shard')
- out_bias_grad: float32 [768], P('shard')
- ln2_gain_grad: float32 [768], P('shard')
- ln2_bias_grad: float32 [768], P('shard')
- up_weight_grad: float32 [768, 3072], P('shard')
- up_bias_grad: float32 [3072], P('shard')
- down_weight_grad: float32 [3072, 768], P('shard')
- down_bias_grad: float32 [768], P('shard')
Inputs may be any that keep to these rules, and one draw needn't show every extreme that they name: `picture_lengths`: each row's pictures lie end to end from position 0; slots after a row's last picture have length 0 and offset 2048; every picture has 100 to 1024 patches; one row holds a picture of 1024, another 20 pictures of 100. `picture_offsets`: the first position of each picture in its row; 2048 for empty slots. `picture_ids`: each patch names the slot of the picture that holds it; a padding slot names the slot after the row's last picture, at most 19. `padding`: 1 exactly on the positions covered by the row's pictures.
All inputs are finite; a program needn't handle non-finite values.
Results may differ from a plain program's by a relative error of at most 0.019.
Values may be sent and summed in bfloat16 or wider, within the bound.
No kernel may reach another device: no remote copies, remote signals or barrier semaphores. Data moves between devices by JAX's collectives and lax.ppermute only.
A program may use at most 320 MiB of HBM per device.

v0:
```python
from functools import partial

import jax
import jax.numpy as jnp
from jax import lax
from jax.sharding import PartitionSpec as P

HEADS = 12
HD = 64


NEG_FILL = -1e30
NORM_EPS = 1e-06


def layer_norm(values, gain_vec, shift_vec):
    center = values - jnp.mean(values, axis=-1, keepdims=True)
    spread = jnp.mean(center * center, axis=-1, keepdims=True)
    return center * lax.rsqrt(spread + NORM_EPS) * gain_vec + shift_vec


def head_norm(values, gain_vec):
    center = values - jnp.mean(values, axis=-1, keepdims=True)
    spread = jnp.mean(center * center, axis=-1, keepdims=True)
    return center * lax.rsqrt(spread + NORM_EPS) * gain_vec


def scaled_norm(values, gain_vec):
    return head_norm(values, gain_vec) * HD ** (-0.5)


def windows(row_ids, row_lengths, row_offsets):
    slot_ids = jnp.arange(row_lengths.shape[-1], dtype=jnp.int32)
    matches = row_ids[..., :, None] == slot_ids
    window_start = jnp.sum(jnp.where(matches, row_offsets[..., None, :], 0), axis=-1)
    window_stop = window_start + jnp.sum(jnp.where(matches, row_lengths[..., None, :], 0), axis=-1)
    return (window_start, window_stop)


def allowed_block(first_row, start_blk, stop_blk, live_blk, live_row):
    key_pos = jnp.arange(live_row.shape[0], dtype=jnp.int32)
    query_pos = first_row + jnp.arange(start_blk.shape[0], dtype=jnp.int32)
    inside = (key_pos[None, :] >= start_blk[:, None]) & (key_pos[None, :] < stop_blk[:, None])
    living = (live_blk[:, None] > 0) & (live_row[None, :] > 0)
    return inside & living | (key_pos[None, :] == query_pos[:, None])


def block_coords(block_index, block_count, group_count, block_rows, group_size):
    row_index = block_index // (block_count * group_count)
    first_row = block_index // group_count % block_count * block_rows
    head_first = block_index % group_count * group_size
    return (row_index, first_row, head_first)


def head_slice(tensor, row_index, start_row, head_first, length, group_size):
    zero_index = jnp.zeros((), jnp.int32)
    return lax.dynamic_slice(
        tensor,
        (row_index, start_row, head_first, zero_index),
        (1, length, group_size, tensor.shape[3]),
    )[0]


def block_scores(query_blk, key_blk, window_start, window_stop, live_rows, row_index, first_row):
    block_rows = query_blk.shape[0]
    start_blk = lax.dynamic_slice(window_start, (row_index, first_row), (1, block_rows))[0]
    stop_blk = lax.dynamic_slice(window_stop, (row_index, first_row), (1, block_rows))[0]
    live_blk = lax.dynamic_slice(live_rows, (row_index, first_row), (1, block_rows))[0]
    live_row = live_rows[0]
    allowed = allowed_block(first_row, start_blk, stop_blk, live_blk, live_row)
    scores = jnp.einsum("qhd,khd->hqk", query_blk, key_blk, preferred_element_type=jnp.float32)
    return jnp.where(allowed[None], scores, NEG_FILL)


def regroup(pieces, row_count, block_count, group_count):
    block_rows, group_size, head_size = (pieces.shape[1], pieces.shape[2], pieces.shape[3])
    shaped = pieces.reshape(row_count, block_count, group_count, block_rows, group_size, head_size)
    shaped = shaped.transpose(0, 1, 3, 2, 4, 5)
    return shaped.reshape(row_count * block_count * block_rows, group_count * group_size, head_size)


def attention_forward(
    queries, key_heads, values, window_start, window_stop, live_rows, block_rows, group_size
):
    row_count, tok_count, head_count, head_size = queries.shape
    block_count = tok_count // block_rows
    group_count = head_count // group_size
    zero_index = jnp.zeros((), jnp.int32)

    def one_piece(block_index):
        row_index, first_row, head_first = block_coords(
            block_index, block_count, group_count, block_rows, group_size
        )
        query_blk = head_slice(queries, row_index, first_row, head_first, block_rows, group_size)
        key_blk = head_slice(key_heads, row_index, zero_index, head_first, tok_count, group_size)
        value_blk = head_slice(values, row_index, zero_index, head_first, tok_count, group_size)
        scores = block_scores(
            query_blk, key_blk, window_start, window_stop, live_rows, row_index, first_row
        )
        row_max = jnp.max(scores, axis=-1, keepdims=True)
        exponent = jnp.exp(scores - row_max)
        denominator = jnp.sum(exponent, axis=-1, keepdims=True)
        shares = (exponent / denominator).astype(jnp.bfloat16)
        attended_blk = jnp.einsum(
            "hqk,khd->qhd", shares, value_blk, preferred_element_type=jnp.float32
        )
        return (attended_blk, row_max[..., 0] + jnp.log(denominator[..., 0]))

    counters = jnp.arange(row_count * block_count * group_count, dtype=jnp.int32)
    pieces, log_totals = lax.map(one_piece, counters)
    attended = regroup(pieces, row_count, block_count, group_count)
    return (attended.reshape(row_count * tok_count, head_count * head_size), log_totals)


def attention_backward(
    queries,
    key_heads,
    values,
    grad_mixed,
    log_totals,
    window_start,
    window_stop,
    live_rows,
    block_rows,
    group_size,
):
    row_count, tok_count, head_count, head_size = queries.shape
    block_count = tok_count // block_rows
    group_count = head_count // group_size
    zero_index = jnp.zeros((), jnp.int32)
    size_tuple = (1, tok_count, group_size, head_size)

    def one_step(carried, block_index):
        key_sum, value_sum = carried
        row_index, first_row, head_first = block_coords(
            block_index, block_count, group_count, block_rows, group_size
        )
        query_blk = head_slice(queries, row_index, first_row, head_first, block_rows, group_size)
        key_blk = head_slice(key_heads, row_index, zero_index, head_first, tok_count, group_size)
        value_blk = head_slice(values, row_index, zero_index, head_first, tok_count, group_size)
        grad_blk = head_slice(grad_mixed, row_index, first_row, head_first, block_rows, group_size)
        scores = block_scores(
            query_blk, key_blk, window_start, window_stop, live_rows, row_index, first_row
        )
        probabilities = jnp.exp(scores - log_totals[block_index][..., None])
        shares = probabilities.astype(jnp.bfloat16)
        grad_shares = jnp.einsum(
            "qhd,khd->hqk", grad_blk, value_blk, preferred_element_type=jnp.float32
        )
        inner_sum = jnp.sum(probabilities * grad_shares, axis=-1, keepdims=True)
        grad_scores = (probabilities * (grad_shares - inner_sum)).astype(jnp.bfloat16)
        grad_query = jnp.einsum(
            "hqk,khd->qhd", grad_scores, key_blk, preferred_element_type=jnp.float32
        )
        grad_key = jnp.einsum(
            "hqk,qhd->khd", grad_scores, query_blk, preferred_element_type=jnp.float32
        )
        grad_value = jnp.einsum(
            "hqk,qhd->khd", shares, grad_blk, preferred_element_type=jnp.float32
        )
        corner = (row_index, zero_index, head_first, zero_index)
        key_sum = lax.dynamic_update_slice(
            key_sum, lax.dynamic_slice(key_sum, corner, size_tuple) + grad_key[None], corner
        )
        value_sum = lax.dynamic_update_slice(
            value_sum, lax.dynamic_slice(value_sum, corner, size_tuple) + grad_value[None], corner
        )
        return ((key_sum, value_sum), grad_query)

    zeros_all = jnp.zeros((row_count, tok_count, head_count, head_size), jnp.float32)
    counters = jnp.arange(row_count * block_count * group_count, dtype=jnp.int32)
    (key_sum, value_sum), query_pieces = lax.scan(one_step, (zeros_all, zeros_all), counters)
    grad_queries = regroup(query_pieces, row_count, block_count, group_count)
    token_total = row_count * tok_count
    return (
        grad_queries,
        key_sum.reshape(token_total, head_count, head_size),
        value_sum.reshape(token_total, head_count, head_size),
    )


def on_device(
    inputs,
    cotangent,
    picture_ids,
    picture_lengths,
    picture_offsets,
    padding,
    ln1_gain,
    ln1_bias,
    qkv_weight,
    qkv_bias,
    query_gain,
    key_gain,
    out_weight,
    out_bias,
    ln2_gain,
    ln2_bias,
    up_weight,
    up_bias,
    down_weight,
    down_bias,
):
    gathered = (
        lax.all_gather(ln1_gain, "shard", axis=0, tiled=True),
        lax.all_gather(ln1_bias, "shard", axis=0, tiled=True),
        lax.all_gather(qkv_weight, "shard", axis=0, tiled=True),
        lax.all_gather(qkv_bias, "shard", axis=0, tiled=True),
        lax.all_gather(query_gain, "shard", axis=0, tiled=True),
        lax.all_gather(key_gain, "shard", axis=0, tiled=True),
        lax.all_gather(out_weight, "shard", axis=0, tiled=True),
        lax.all_gather(out_bias, "shard", axis=0, tiled=True),
        lax.all_gather(ln2_gain, "shard", axis=0, tiled=True),
        lax.all_gather(ln2_bias, "shard", axis=0, tiled=True),
        lax.all_gather(up_weight, "shard", axis=0, tiled=True),
        lax.all_gather(up_bias, "shard", axis=0, tiled=True),
        lax.all_gather(down_weight, "shard", axis=0, tiled=True),
        lax.all_gather(down_bias, "shard", axis=0, tiled=True),
    )
    (
        gain_one,
        shift_one,
        weight_qkv,
        bias_qkv,
        gain_query,
        gain_key,
        weight_out,
        bias_out,
        gain_two,
        shift_two,
        weight_up,
        bias_up,
        weight_down,
        bias_down,
    ) = gathered
    row_count = picture_lengths.shape[0]
    token_total = inputs.shape[0]
    tok_count = token_total // row_count
    block_rows = min(512, tok_count)
    group_size = 4
    live_rows = padding.reshape(row_count, tok_count)
    window_start, window_stop = windows(
        picture_ids.reshape(row_count, tok_count), picture_lengths, picture_offsets
    )
    float32 = jnp.float32
    bfloat = jnp.bfloat16
    input_float = inputs.astype(float32)
    gain_one_f, shift_one_f = (gain_one.astype(float32), shift_one.astype(float32))
    normed = layer_norm(input_float, gain_one_f, shift_one_f)
    normed_low = normed.astype(bfloat)
    qkv_all = jnp.dot(normed_low, weight_qkv, preferred_element_type=float32) + bias_qkv.astype(
        float32
    )
    head_view = qkv_all.reshape(token_total, 3, HEADS, HD)
    query_pre = head_view[:, 0]
    key_pre = head_view[:, 1]
    queries = (
        scaled_norm(query_pre, gain_query.astype(float32))
        .astype(bfloat)
        .reshape(row_count, tok_count, HEADS, HD)
    )
    key_heads = (
        head_norm(key_pre, gain_key.astype(float32))
        .astype(bfloat)
        .reshape(row_count, tok_count, HEADS, HD)
    )
    values = head_view[:, 2].astype(bfloat).reshape(row_count, tok_count, HEADS, HD)
    attended, log_totals = attention_forward(
        queries, key_heads, values, window_start, window_stop, live_rows, block_rows, group_size
    )
    mixed_low = attended.astype(bfloat)
    hidden = (
        input_float
        + jnp.dot(mixed_low, weight_out, preferred_element_type=float32)
        + bias_out.astype(float32)
    )
    normed_two = layer_norm(hidden, gain_two.astype(float32), shift_two.astype(float32))
    normed_two_low = normed_two.astype(bfloat)
    up_proj = jnp.dot(normed_two_low, weight_up, preferred_element_type=float32) + bias_up.astype(
        float32
    )
    activated = jax.nn.gelu(up_proj, approximate=False).astype(bfloat)
    output = (
        hidden
        + jnp.dot(activated, weight_down, preferred_element_type=float32)
        + bias_down.astype(float32)
    ).astype(bfloat)
    (
        gain_one,
        shift_one,
        weight_qkv,
        bias_qkv,
        gain_query,
        gain_key,
        weight_out,
        bias_out,
        gain_two,
        shift_two,
        weight_up,
        bias_up,
        weight_down,
        bias_down,
    ) = (
        lax.all_gather(ln1_gain, "shard", axis=0, tiled=True),
        lax.all_gather(ln1_bias, "shard", axis=0, tiled=True),
        lax.all_gather(qkv_weight, "shard", axis=0, tiled=True),
        lax.all_gather(qkv_bias, "shard", axis=0, tiled=True),
        lax.all_gather(query_gain, "shard", axis=0, tiled=True),
        lax.all_gather(key_gain, "shard", axis=0, tiled=True),
        lax.all_gather(out_weight, "shard", axis=0, tiled=True),
        lax.all_gather(out_bias, "shard", axis=0, tiled=True),
        lax.all_gather(ln2_gain, "shard", axis=0, tiled=True),
        lax.all_gather(ln2_bias, "shard", axis=0, tiled=True),
        lax.all_gather(up_weight, "shard", axis=0, tiled=True),
        lax.all_gather(up_bias, "shard", axis=0, tiled=True),
        lax.all_gather(down_weight, "shard", axis=0, tiled=True),
        lax.all_gather(down_bias, "shard", axis=0, tiled=True),
    )
    grad_out = cotangent.astype(float32) * padding.astype(float32)[:, None]
    grad_mlp = grad_out.astype(bfloat)
    grad_bias_down = jnp.sum(grad_mlp, axis=0, dtype=float32)
    grad_weight_down = jnp.einsum("tf,td->fd", activated, grad_mlp, preferred_element_type=float32)
    grad_act = jnp.einsum("td,fd->tf", grad_mlp, weight_down, preferred_element_type=float32)
    _, gelu_back = jax.vjp(partial(jax.nn.gelu, approximate=False), up_proj)
    grad_up = gelu_back(grad_act)[0].astype(bfloat)
    grad_bias_up = jnp.sum(grad_up, axis=0, dtype=float32)
    grad_weight_up = jnp.einsum(
        "td,tf->df", normed_two_low, grad_up, preferred_element_type=float32
    )
    grad_norm_two = jnp.einsum("tf,df->td", grad_up, weight_up, preferred_element_type=float32)
    _, norm_two_back = jax.vjp(
        layer_norm, hidden, gain_two.astype(float32), shift_two.astype(float32)
    )
    hidden_part, grad_gain_two, grad_shift_two = norm_two_back(grad_norm_two)
    grad_hidden = grad_out + hidden_part
    grad_branch = grad_hidden.astype(bfloat)
    grad_bias_out = jnp.sum(grad_branch, axis=0, dtype=float32)
    grad_weight_out = jnp.einsum(
        "td,te->de", mixed_low, grad_branch, preferred_element_type=float32
    )
    grad_mixed = jnp.einsum("te,de->td", grad_branch, weight_out, preferred_element_type=float32)
    grad_mixed = grad_mixed.astype(bfloat).reshape(row_count, tok_count, HEADS, HD)
    grad_queries, grad_keys, grad_values = attention_backward(
        queries,
        key_heads,
        values,
        grad_mixed,
        log_totals,
        window_start,
        window_stop,
        live_rows,
        block_rows,
        group_size,
    )
    _, query_back = jax.vjp(scaled_norm, query_pre, gain_query.astype(float32))
    grad_q_pre, grad_gain_query = query_back(grad_queries)
    _, key_back = jax.vjp(head_norm, key_pre, gain_key.astype(float32))
    grad_k_pre, grad_gain_key = key_back(grad_keys)
    grad_qkv = jnp.stack([grad_q_pre, grad_k_pre, grad_values], axis=1).reshape(
        token_total, 3 * HEADS * HD
    )
    grad_qkv = grad_qkv.astype(bfloat)
    grad_bias_qkv = jnp.sum(grad_qkv, axis=0, dtype=float32)
    grad_weight_qkv = jnp.einsum("td,te->de", normed_low, grad_qkv, preferred_element_type=float32)
    grad_normed = jnp.einsum("te,de->td", grad_qkv, weight_qkv, preferred_element_type=float32)
    _, norm_one_back = jax.vjp(
        layer_norm, input_float, gain_one.astype(float32), shift_one.astype(float32)
    )
    input_part, grad_gain_one, grad_shift_one = norm_one_back(grad_normed)
    input_grad = grad_hidden + input_part
    owned_all = (
        lax.psum_scatter(
            grad_gain_one.astype(jnp.bfloat16), "shard", scatter_dimension=0, tiled=True
        ).astype(jnp.float32),
        lax.psum_scatter(
            grad_shift_one.astype(jnp.bfloat16), "shard", scatter_dimension=0, tiled=True
        ).astype(jnp.float32),
        lax.psum_scatter(
            grad_weight_qkv.astype(jnp.bfloat16), "shard", scatter_dimension=0, tiled=True
        ).astype(jnp.float32),
        lax.psum_scatter(
            grad_bias_qkv.astype(jnp.bfloat16), "shard", scatter_dimension=0, tiled=True
        ).astype(jnp.float32),
        lax.psum_scatter(
            grad_gain_query.astype(jnp.bfloat16), "shard", scatter_dimension=0, tiled=True
        ).astype(jnp.float32),
        lax.psum_scatter(
            grad_gain_key.astype(jnp.bfloat16), "shard", scatter_dimension=0, tiled=True
        ).astype(jnp.float32),
        lax.psum_scatter(
            grad_weight_out.astype(jnp.bfloat16), "shard", scatter_dimension=0, tiled=True
        ).astype(jnp.float32),
        lax.psum_scatter(
            grad_bias_out.astype(jnp.bfloat16), "shard", scatter_dimension=0, tiled=True
        ).astype(jnp.float32),
        lax.psum_scatter(
            grad_gain_two.astype(jnp.bfloat16), "shard", scatter_dimension=0, tiled=True
        ).astype(jnp.float32),
        lax.psum_scatter(
            grad_shift_two.astype(jnp.bfloat16), "shard", scatter_dimension=0, tiled=True
        ).astype(jnp.float32),
        lax.psum_scatter(
            grad_weight_up.astype(jnp.bfloat16), "shard", scatter_dimension=0, tiled=True
        ).astype(jnp.float32),
        lax.psum_scatter(
            grad_bias_up.astype(jnp.bfloat16), "shard", scatter_dimension=0, tiled=True
        ).astype(jnp.float32),
        lax.psum_scatter(
            grad_weight_down.astype(jnp.bfloat16), "shard", scatter_dimension=0, tiled=True
        ).astype(jnp.float32),
        lax.psum_scatter(
            grad_bias_down.astype(jnp.bfloat16), "shard", scatter_dimension=0, tiled=True
        ).astype(jnp.float32),
    )
    (
        owned_gain_one,
        owned_shift_one,
        owned_weight_qkv,
        owned_bias_qkv,
        owned_gain_query,
        owned_gain_key,
        owned_weight_out,
        owned_bias_out,
        owned_gain_two,
        owned_shift_two,
        owned_weight_up,
        owned_bias_up,
        owned_weight_down,
        owned_bias_down,
    ) = owned_all
    finished = tuple(
        (
            lax.psum(owned_gain_one.astype(jnp.bfloat16), "rep").astype(jnp.float32),
            lax.psum(owned_shift_one.astype(jnp.bfloat16), "rep").astype(jnp.float32),
            lax.psum(owned_weight_qkv.astype(jnp.bfloat16), "rep").astype(jnp.float32),
            lax.psum(owned_bias_qkv.astype(jnp.bfloat16), "rep").astype(jnp.float32),
            lax.psum(owned_gain_query.astype(jnp.bfloat16), "rep").astype(jnp.float32),
            lax.psum(owned_gain_key.astype(jnp.bfloat16), "rep").astype(jnp.float32),
            lax.psum(owned_weight_out.astype(jnp.bfloat16), "rep").astype(jnp.float32),
            lax.psum(owned_bias_out.astype(jnp.bfloat16), "rep").astype(jnp.float32),
            lax.psum(owned_gain_two.astype(jnp.bfloat16), "rep").astype(jnp.float32),
            lax.psum(owned_shift_two.astype(jnp.bfloat16), "rep").astype(jnp.float32),
            lax.psum(owned_weight_up.astype(jnp.bfloat16), "rep").astype(jnp.float32),
            lax.psum(owned_bias_up.astype(jnp.bfloat16), "rep").astype(jnp.float32),
            lax.psum(owned_weight_down.astype(jnp.bfloat16), "rep").astype(jnp.float32),
            lax.psum(owned_bias_down.astype(jnp.bfloat16), "rep").astype(jnp.float32),
        )
    )
    return (output, input_grad) + finished


def solution(mesh):
    in_specs = (
        P(("rep", "shard"), None),
        P(("rep", "shard"), None),
        P(("rep", "shard")),
        P(("rep", "shard"), None),
        P(("rep", "shard"), None),
        P(("rep", "shard")),
        P("shard"),
        P("shard"),
        P("shard", None),
        P("shard"),
        P("shard"),
        P("shard"),
        P("shard", None),
        P("shard"),
        P("shard"),
        P("shard"),
        P("shard", None),
        P("shard"),
        P("shard", None),
        P("shard"),
    )
    out_specs = (
        P(("rep", "shard"), None),
        P(("rep", "shard"), None),
        P("shard"),
        P("shard"),
        P("shard", None),
        P("shard"),
        P("shard"),
        P("shard"),
        P("shard", None),
        P("shard"),
        P("shard"),
        P("shard"),
        P("shard", None),
        P("shard"),
        P("shard", None),
        P("shard"),
    )
    return jax.shard_map(
        on_device, mesh=mesh, in_specs=in_specs, out_specs=out_specs, check_vma=False
    )
```

profile of v0, /device:TPU:0, one launch (start us, length us, event | category | flops | bytes accessed | tf_op | source)
XLA Modules:
  0.0 1726.6 jit_solution(530438782381214430)
XLA Ops:
  22.1 26.1 %all-reduce.20 = (bf16[2304]{0:T(1024)(128)(2,1)S(1)}, bf16[768]{0:T(1024)(128)(2,1)S(1)}, bf16[768]{0:T(1024)(128)(2,1)S(1)}, bf16[64]{0:T(256)(128)(2,1)S(1)},...) all-reduce(bf16[2304]{0:T(1024)(128)(2,1)S(1)} %dynamic-update-slic, ...), channel_id=1, replica_groups=mesh['rep'=4,'shard'=8] {'shard'}, use_global_device_ids=true, to_apply=%add.2 | all-reduce | flops 6272 | bytes 25088
  55.3 8.3 all-gather
  70.0 14.0 convolution_add_fusion
  83.9 18.8 %copy.81 = f32[2048,2304]{0,1:T(8,128)} copy(f32[2048,2304]{1,0:T(8,128)} %convolution_add_fusion) | data formatting | bytes 37748736 | tf_op jit(solution)/shard_map/add | solution.py:251
  102.7 9.2 slice_reduce_fusion
  123.8 7.7 fusion.86
  131.6 248.2 %while.34 = (s32[]{:T(128)}, bf16[12,512,4,64]{1,3,2,0:T(8,128)(2,1)}, f32[12,4,512]{2,1,0:T(4,128)}, s32[12]{0:T(128)S(1)}, bf16[1,2048,12,64]{1,3,2,0:T(8,128)...) while((s32[]{:T(128)}, ...), condition=%wide.region_11.12_spmd.clone, body=%wide.region_8.11_spmd.sunk.clone | while | flops 1118831616 | bytes 57509836 | solution.py:110
  396.2 8.4 squeeze.86
  410.1 68.2 %multiply_convert_fusion.1 = (bf16[2048,3072]{1,0:T(8,128)(2,1)}, f32[2048,3072]{1,0:T(8,128)}, f32[2048,3072]{1,0:T(8,128)}) fusion(f32[3072]{0:T(1024)S(1)} %bitcast.309, bf16[768,3072]{1,0:T(8,128)(2,1)} %all-gather.10.cloned.1.call-done, bf16[2048,768]{0,1:T(8,128)(2,1)} %add_convert_fusion.4.clone.4), kind=kOutput, calls=%fused_computation.83 | convolution fusion | flops 10078912512 | bytes 70791168 | tf_op jit(solution)/shard_map/dot_general | solution.py:279
  478.3 28.9 %fusion.117 = (bf16[3072]{0:T(1024)(128)(2,1)}, bf16[2048,3072]{1,0:T(8,128)(2,1)}) fusion(f32[2048,3072]{1,0:T(8,128)} %get-tuple-element.558, bf16[3072,768]{1,0:T(8,128)(2,1)} %all-gather.12.cloned.1.call-done, bf16[2048,768]{0,1:T(8,128)(2,1)S(1)} %copy-done.7, f32[2048]{0:T(1024)S(1)} %copy-done.42, f32[2048,3072]{1,0:T(8,128)} %get-tuple-element.581, ...), kind=kOutput, calls=%fused_computation.202 | convolution fusion | flops 9769055232 | bytes 70805504 | tf_op jit(solution)/shard_map/td,fd->tf/dot_general | solution.py:323
  507.2 15.2 fusion.116
  552.8 820.1 %while.35 = (s32[]{:T(128)}, f32[1,2048,12,64]{1,3,2,0:T(8,128)}, f32[1,2048,12,64]{1,3,2,0:T(8,128)}, f32[12,512,4,64]{1,3,2,0:T(8,128)}, s32[12]{0:T(128)S(1)}...) while((s32[]{:T(128)}, f32[1,2048,12,64]{1,3,2,0:T(8,128)}, ...), condition=%wide.region_18.19_spmd.clone, body=%wide.region_16.18_spmd.sunk.clone | while | flops 2743075840 | bytes 193558608 | solution.py:172
  555.5 9.4 fusion.186
  571.1 12.3 multiply_reduce_fusion.11
  583.4 16.0 multiply_convert_fusion.4
  624.0 9.4 fusion.186
  639.5 12.3 multiply_reduce_fusion.11
  651.8 16.0 multiply_convert_fusion.4
  692.2 9.4 fusion.186
  707.8 12.3 multiply_reduce_fusion.11
  720.1 16.0 multiply_convert_fusion.4
  760.5 9.4 fusion.186
  776.0 12.3 multiply_reduce_fusion.11
  788.3 16.0 multiply_convert_fusion.4
  828.9 9.4 fusion.186
  844.4 12.3 multiply_reduce_fusion.11
  856.7 16.0 multiply_convert_fusion.4
  897.1 9.4 fusion.186
  912.6 12.3 multiply_reduce_fusion.11
  924.9 16.0 multiply_convert_fusion.4
  965.3 9.4 fusion.186
  980.9 12.3 multiply_reduce_fusion.11
  993.2 16.0 multiply_convert_fusion.4
  1033.8 9.4 fusion.186
  1049.3 12.3 multiply_reduce_fusion.11
  1061.6 16.0 multiply_convert_fusion.4
  1102.0 9.4 fusion.186
  1117.6 12.3 multiply_reduce_fusion.11
  1129.9 16.0 multiply_convert_fusion.4
  1170.3 9.4 fusion.186
  1185.8 12.3 multiply_reduce_fusion.11
  1198.1 16.0 multiply_convert_fusion.4
  1228.5 7.6 fusion.189
  1238.7 9.4 fusion.186
  1254.1 12.3 multiply_reduce_fusion.11
  1266.5 16.0 multiply_convert_fusion.4
  1306.9 9.4 fusion.186
  1322.3 12.3 multiply_reduce_fusion.11
  1334.7 16.0 multiply_convert_fusion.4
  1386.3 8.5 reshape.720
  1394.9 11.1 fusion.82
  1406.1 8.6 reshape.719
  1421.4 9.0 fusion.79
  1430.7 11.1 fusion.78
  1449.4 13.4 convolution_convert_fusion.2
  1462.9 16.5 convolution_convert_fusion.1
  1479.5 16.2 convolution_convert_fusion
  1498.9 13.0 fusion.115
  1526.4 23.9 %all-reduce.19 = (bf16[768]{0:T(1024)(128)(2,1)S(1)}, bf16[768]{0:T(1024)(128)(2,1)S(1)}, bf16[768]{0:T(1024)(128)(2,1)S(1)}, bf16[2304]{0:T(1024)(128)(2,1)S(1)...) all-reduce(bf16[768]{0:T(1024)(128)(2,1)S(1)} %dynamic-update-slice, ...), channel_id=1, replica_groups=mesh['rep'=4,'shard'=8] {'shard'}, use_global_device_ids=true, to_apply=%add.8 | all-reduce | flops 10880 | bytes 43520
  1551.1 12.5 all-reduce.21
  1568.8 8.9 add_add_fusion.6
  1584.3 49.5 %reduce-scatter.11.cloned.1.call-done = bf16[384,768]{1,0:T(8,128)(2,1)} async-done(((bf16[3072,768]{1,0:T(8,128)(2,1)}), bf16[384,768]{1,0:T(8,128)(2,1)}) %reduce-scatter.11.cloned.1.call-update) | async-done | bytes 589840 | tf_op jit(solution)/shard_map/reduce_scatter | solution.py:408
  1633.8 15.3 add_convert_fusion.1
  1651.9 60.1 %all-reduce.25.cloned.1.call-done = (bf16[96,2304]{1,0:T(8,128)(2,1)}, bf16[96,768]{1,0:T(8,128)(2,1)}, bf16[96,3072]{1,0:T(8,128)(2,1)}, bf16[384,768]{1,0:T(8,128)(2,1)}) async-done(((bf16[96,2304]{1,0:T(8,128)(2,1)}, bf16[96,768]{1,0:T(8,128)(2,1)}, bf16[96,3072]{1,0:T(8,128)(2,1)}, bf16[384,768]{1,0:T(8,128)(2,1)}), (bf16[96,2304]{1,0:T(8,128)(2,1)}, bf16[96,768]{1,0:T(8,128)(2,1)}, ...) | async-done | bytes 1769488 | tf_op jit(solution)/shard_map/psum | solution.py:435
  (633 shorter events, 691.1 us)
Async XLA Ops:
  7.2 62.7 %all-gather.6.cloned.1.call-start = ((), (), s32[]{:S(2)}) async-start(), calls=%async_computation.4 | async-start | bytes 3981312 | tf_op jit(solution)/shard_map/all_gather | solution.py:207
  7.9 379.1 %all-gather.8.cloned.1.call-start = ((), (), s32[]{:S(2)}) async-start(), calls=%async_computation.5 | async-start | bytes 1327104 | tf_op jit(solution)/shard_map/all_gather | solution.py:211
  8.7 401.4 %all-gather.10.cloned.1.call-start = ((), (), s32[]{:S(2)}) async-start(), calls=%async_computation.6 | async-start | bytes 5308416 | tf_op jit(solution)/shard_map/all_gather | solution.py:215
  9.4 468.9 %all-gather.12.cloned.1.call-start = ((), (), s32[]{:S(2)}) async-start(), calls=%async_computation.7 | async-start | bytes 5308416 | tf_op jit(solution)/shard_map/all_gather | solution.py:217
  10.0 1574.3 %reduce-scatter.7.cloned.1.call-start = ((), (), s32[]{:S(2)}) async-start(), calls=%async_computation.9 | async-start | bytes 1327104 | tf_op jit(solution)/shard_map/reduce_scatter | solution.py:390
  48.8 21.2 %copy-start.46 = (f32[768]{0:T(1024)}, f32[768]{0:T(1024)S(1)}, u32[]{:S(2)}) copy-start(f32[768]{0:T(1024)S(1)} %convert_element_type.247) | copy-start | bytes 9220
  48.8 21.2 %copy-start.62 = (f32[768]{0:T(1024)}, f32[768]{0:T(1024)S(1)}, u32[]{:S(2)}) copy-start(f32[768]{0:T(1024)S(1)} %convert_element_type.248) | copy-start | bytes 9220
  52.0 18.0 %copy-start = (bf16[2048,768]{0,1:T(8,128)(2,1)}, bf16[2048,768]{0,1:T(8,128)(2,1)S(1)}, u32[]{:S(2)}) copy-start(bf16[2048,768]{0,1:T(8,128)(2,1)S(1)} %copy.80) | copy-start | bytes 9437188
  52.0 16.9 copy-start.19
  52.0 17.5 %copy-start.58 = (s32[2048]{0:T(1024)S(1)}, s32[2048]{0:T(1024)}, u32[]{:S(2)}) copy-start(s32[2048]{0:T(1024)} %param.26) | copy-start | bytes 24580
  52.0 17.4 %copy-start.67 = (s32[1,20]{1,0:T(1,128)S(1)}, s32[1,20]{1,0:T(1,128)}, u32[]{:S(2)}) copy-start(s32[1,20]{1,0:T(1,128)} %param.27) | copy-start | bytes 244
  52.0 17.4 %copy-start.68 = (s32[1,20]{1,0:T(1,128)S(1)}, s32[1,20]{1,0:T(1,128)}, u32[]{:S(2)}) copy-start(s32[1,20]{1,0:T(1,128)} %param.28) | copy-start | bytes 244
  52.5 31.4 %copy-start.26 = (f32[2048]{0:T(1024)}, f32[2048]{0:T(1024)S(1)}, u32[]{:S(2)}) copy-start(f32[2048]{0:T(1024)S(1)} %broadcast_multiply_fusion.3) | copy-start | bytes 24580
  53.4 16.0 copy-start.38
  53.4 30.5 %copy-start.36 = (f32[2048]{0:T(1024)}, f32[2048]{0:T(1024)S(1)}, u32[]{:S(2)}) copy-start(f32[2048]{0:T(1024)S(1)} %fusion.101) | copy-start | bytes 24580
  53.5 70.3 %copy-start.54 = (f32[64]{0:T(128)}, f32[64]{0:T(128)S(1)}, u32[]{:S(2)}) copy-start(f32[64]{0:T(128)S(1)} %convert_element_type.254) | copy-start | bytes 772
  410.1 68.2 %copy-start.7 = (bf16[2048,768]{0,1:T(8,128)(2,1)S(1)}, bf16[2048,768]{0,1:T(8,128)(2,1)}, u32[]{:S(2)}) copy-start(bf16[2048,768]{0,1:T(8,128)(2,1)} %copy.84) | copy-start | bytes 9437188
  410.1 68.2 %copy-start.42 = (f32[2048]{0:T(1024)S(1)}, f32[2048]{0:T(1024)}, u32[]{:S(2)}) copy-start(f32[2048]{0:T(1024)} %convert_element_type.269) | copy-start | bytes 24580
  478.3 28.9 %copy-start.69 = (bf16[768,3072]{1,0:T(8,128)(2,1)S(1)}, bf16[768,3072]{1,0:T(8,128)(2,1)}, u32[]{:S(2)}) copy-start(bf16[768,3072]{1,0:T(8,128)(2,1)} %all-gather.10.cloned.1.call-done) | copy-start | bytes 14155780
  552.8 820.1 %copy-start.11 = (f32[2048,12]{0,1:T(8,128)S(1)}, f32[2048,12]{0,1:T(8,128)}, u32[]{:S(2)}) copy-start(f32[2048,12]{0,1:T(8,128)} %copy-done.10) | copy-start | bytes 294916
  552.8 820.1 %copy-start.55 = (f32[64]{0:T(128)S(1)}, f32[64]{0:T(128)}, u32[]{:S(2)}) copy-start(f32[64]{0:T(128)} %copy-done.54) | copy-start | bytes 772
  583.4 30.4 %slice-start = ((s8[16777216]{0:T(1024)(128)(4,1)}), s8[4194304]{0:T(1024)(128)(4,1)S(1)}, s32[]{:S(2)}) async-start(s8[16777216]{0:T(1024)(128)(4,1)} %bitcast.275), calls=%async_computation.13 | async-start | bytes 8388608 | tf_op jit(solution)/shard_map/while
  583.4 30.4 %slice-start.1 = ((s8[16777216]{0:T(1024)(128)(4,1)}), s8[4194304]{0:T(1024)(128)(4,1)S(1)}, s32[]{:S(2)}) async-start(s8[16777216]{0:T(1024)(128)(4,1)} %bitcast.275), calls=%async_computation.14 | async-start | bytes 8388608 | tf_op jit(solution)/shard_map/while
  583.4 30.4 %slice-start.2 = ((s8[16777216]{0:T(1024)(128)(4,1)}), s8[4194304]{0:T(1024)(128)(4,1)S(1)}, s32[]{:S(2)}) async-start(s8[16777216]{0:T(1024)(128)(4,1)} %bitcast.275), calls=%async_computation.15 | async-start | bytes 8388608 | tf_op jit(solution)/shard_map/while
  651.8 30.4 %slice-start = ((s8[16777216]{0:T(1024)(128)(4,1)}), s8[4194304]{0:T(1024)(128)(4,1)S(1)}, s32[]{:S(2)}) async-start(s8[16777216]{0:T(1024)(128)(4,1)} %bitcast.275), calls=%async_computation.13 | async-start | bytes 8388608 | tf_op jit(solution)/shard_map/while
  651.8 30.4 %slice-start.1 = ((s8[16777216]{0:T(1024)(128)(4,1)}), s8[4194304]{0:T(1024)(128)(4,1)S(1)}, s32[]{:S(2)}) async-start(s8[16777216]{0:T(1024)(128)(4,1)} %bitcast.275), calls=%async_computation.14 | async-start | bytes 8388608 | tf_op jit(solution)/shard_map/while
  651.8 30.4 %slice-start.2 = ((s8[16777216]{0:T(1024)(128)(4,1)}), s8[4194304]{0:T(1024)(128)(4,1)S(1)}, s32[]{:S(2)}) async-start(s8[16777216]{0:T(1024)(128)(4,1)} %bitcast.275), calls=%async_computation.15 | async-start | bytes 8388608 | tf_op jit(solution)/shard_map/while
  720.1 30.4 %slice-start = ((s8[16777216]{0:T(1024)(128)(4,1)}), s8[4194304]{0:T(1024)(128)(4,1)S(1)}, s32[]{:S(2)}) async-start(s8[16777216]{0:T(1024)(128)(4,1)} %bitcast.275), calls=%async_computation.13 | async-start | bytes 8388608 | tf_op jit(solution)/shard_map/while
  720.1 30.4 %slice-start.1 = ((s8[16777216]{0:T(1024)(128)(4,1)}), s8[4194304]{0:T(1024)(128)(4,1)S(1)}, s32[]{:S(2)}) async-start(s8[16777216]{0:T(1024)(128)(4,1)} %bitcast.275), calls=%async_computation.14 | async-start | bytes 8388608 | tf_op jit(solution)/shard_map/while
  720.1 30.4 %slice-start.2 = ((s8[16777216]{0:T(1024)(128)(4,1)}), s8[4194304]{0:T(1024)(128)(4,1)S(1)}, s32[]{:S(2)}) async-start(s8[16777216]{0:T(1024)(128)(4,1)} %bitcast.275), calls=%async_computation.15 | async-start | bytes 8388608 | tf_op jit(solution)/shard_map/while
  788.3 30.4 %slice-start = ((s8[16777216]{0:T(1024)(128)(4,1)}), s8[4194304]{0:T(1024)(128)(4,1)S(1)}, s32[]{:S(2)}) async-start(s8[16777216]{0:T(1024)(128)(4,1)} %bitcast.275), calls=%async_computation.13 | async-start | bytes 8388608 | tf_op jit(solution)/shard_map/while
  788.3 30.4 %slice-start.1 = ((s8[16777216]{0:T(1024)(128)(4,1)}), s8[4194304]{0:T(1024)(128)(4,1)S(1)}, s32[]{:S(2)}) async-start(s8[16777216]{0:T(1024)(128)(4,1)} %bitcast.275), calls=%async_computation.14 | async-start | bytes 8388608 | tf_op jit(solution)/shard_map/while
  788.3 30.4 %slice-start.2 = ((s8[16777216]{0:T(1024)(128)(4,1)}), s8[4194304]{0:T(1024)(128)(4,1)S(1)}, s32[]{:S(2)}) async-start(s8[16777216]{0:T(1024)(128)(4,1)} %bitcast.275), calls=%async_computation.15 | async-start | bytes 8388608 | tf_op jit(solution)/shard_map/while
  856.7 30.4 %slice-start = ((s8[16777216]{0:T(1024)(128)(4,1)}), s8[4194304]{0:T(1024)(128)(4,1)S(1)}, s32[]{:S(2)}) async-start(s8[16777216]{0:T(1024)(128)(4,1)} %bitcast.275), calls=%async_computation.13 | async-start | bytes 8388608 | tf_op jit(solution)/shard_map/while
  856.7 30.4 %slice-start.1 = ((s8[16777216]{0:T(1024)(128)(4,1)}), s8[4194304]{0:T(1024)(128)(4,1)S(1)}, s32[]{:S(2)}) async-start(s8[16777216]{0:T(1024)(128)(4,1)} %bitcast.275), calls=%async_computation.14 | async-start | bytes 8388608 | tf_op jit(solution)/shard_map/while
  856.7 30.4 %slice-start.2 = ((s8[16777216]{0:T(1024)(128)(4,1)}), s8[4194304]{0:T(1024)(128)(4,1)S(1)}, s32[]{:S(2)}) async-start(s8[16777216]{0:T(1024)(128)(4,1)} %bitcast.275), calls=%async_computation.15 | async-start | bytes 8388608 | tf_op jit(solution)/shard_map/while
  924.9 30.4 %slice-start = ((s8[16777216]{0:T(1024)(128)(4,1)}), s8[4194304]{0:T(1024)(128)(4,1)S(1)}, s32[]{:S(2)}) async-start(s8[16777216]{0:T(1024)(128)(4,1)} %bitcast.275), calls=%async_computation.13 | async-start | bytes 8388608 | tf_op jit(solution)/shard_map/while
  924.9 30.4 %slice-start.1 = ((s8[16777216]{0:T(1024)(128)(4,1)}), s8[4194304]{0:T(1024)(128)(4,1)S(1)}, s32[]{:S(2)}) async-start(s8[16777216]{0:T(1024)(128)(4,1)} %bitcast.275), calls=%async_computation.14 | async-start | bytes 8388608 | tf_op jit(solution)/shard_map/while
  924.9 30.4 %slice-start.2 = ((s8[16777216]{0:T(1024)(128)(4,1)}), s8[4194304]{0:T(1024)(128)(4,1)S(1)}, s32[]{:S(2)}) async-start(s8[16777216]{0:T(1024)(128)(4,1)} %bitcast.275), calls=%async_computation.15 | async-start | bytes 8388608 | tf_op jit(solution)/shard_map/while
  993.2 30.4 %slice-start = ((s8[16777216]{0:T(1024)(128)(4,1)}), s8[4194304]{0:T(1024)(128)(4,1)S(1)}, s32[]{:S(2)}) async-start(s8[16777216]{0:T(1024)(128)(4,1)} %bitcast.275), calls=%async_computation.13 | async-start | bytes 8388608 | tf_op jit(solution)/shard_map/while
  993.2 30.4 %slice-start.1 = ((s8[16777216]{0:T(1024)(128)(4,1)}), s8[4194304]{0:T(1024)(128)(4,1)S(1)}, s32[]{:S(2)}) async-start(s8[16777216]{0:T(1024)(128)(4,1)} %bitcast.275), calls=%async_computation.14 | async-start | bytes 8388608 | tf_op jit(solution)/shard_map/while
  993.2 30.4 %slice-start.2 = ((s8[16777216]{0:T(1024)(128)(4,1)}), s8[4194304]{0:T(1024)(128)(4,1)S(1)}, s32[]{:S(2)}) async-start(s8[16777216]{0:T(1024)(128)(4,1)} %bitcast.275), calls=%async_computation.15 | async-start | bytes 8388608 | tf_op jit(solution)/shard_map/while
  1061.6 30.4 %slice-start = ((s8[16777216]{0:T(1024)(128)(4,1)}), s8[4194304]{0:T(1024)(128)(4,1)S(1)}, s32[]{:S(2)}) async-start(s8[16777216]{0:T(1024)(128)(4,1)} %bitcast.275), calls=%async_computation.13 | async-start | bytes 8388608 | tf_op jit(solution)/shard_map/while
  1061.6 30.4 %slice-start.1 = ((s8[16777216]{0:T(1024)(128)(4,1)}), s8[4194304]{0:T(1024)(128)(4,1)S(1)}, s32[]{:S(2)}) async-start(s8[16777216]{0:T(1024)(128)(4,1)} %bitcast.275), calls=%async_computation.14 | async-start | bytes 8388608 | tf_op jit(solution)/shard_map/while
  1061.6 30.4 %slice-start.2 = ((s8[16777216]{0:T(1024)(128)(4,1)}), s8[4194304]{0:T(1024)(128)(4,1)S(1)}, s32[]{:S(2)}) async-start(s8[16777216]{0:T(1024)(128)(4,1)} %bitcast.275), calls=%async_computation.15 | async-start | bytes 8388608 | tf_op jit(solution)/shard_map/while
  1129.9 30.4 %slice-start = ((s8[16777216]{0:T(1024)(128)(4,1)}), s8[4194304]{0:T(1024)(128)(4,1)S(1)}, s32[]{:S(2)}) async-start(s8[16777216]{0:T(1024)(128)(4,1)} %bitcast.275), calls=%async_computation.13 | async-start | bytes 8388608 | tf_op jit(solution)/shard_map/while
  1129.9 30.4 %slice-start.1 = ((s8[16777216]{0:T(1024)(128)(4,1)}), s8[4194304]{0:T(1024)(128)(4,1)S(1)}, s32[]{:S(2)}) async-start(s8[16777216]{0:T(1024)(128)(4,1)} %bitcast.275), calls=%async_computation.14 | async-start | bytes 8388608 | tf_op jit(solution)/shard_map/while
  1129.9 30.4 %slice-start.2 = ((s8[16777216]{0:T(1024)(128)(4,1)}), s8[4194304]{0:T(1024)(128)(4,1)S(1)}, s32[]{:S(2)}) async-start(s8[16777216]{0:T(1024)(128)(4,1)} %bitcast.275), calls=%async_computation.15 | async-start | bytes 8388608 | tf_op jit(solution)/shard_map/while
  1198.1 30.4 %slice-start = ((s8[16777216]{0:T(1024)(128)(4,1)}), s8[4194304]{0:T(1024)(128)(4,1)S(1)}, s32[]{:S(2)}) async-start(s8[16777216]{0:T(1024)(128)(4,1)} %bitcast.275), calls=%async_computation.13 | async-start | bytes 8388608 | tf_op jit(solution)/shard_map/while
  1198.1 30.4 %slice-start.1 = ((s8[16777216]{0:T(1024)(128)(4,1)}), s8[4194304]{0:T(1024)(128)(4,1)S(1)}, s32[]{:S(2)}) async-start(s8[16777216]{0:T(1024)(128)(4,1)} %bitcast.275), calls=%async_computation.14 | async-start | bytes 8388608 | tf_op jit(solution)/shard_map/while
  1198.1 30.4 %slice-start.2 = ((s8[16777216]{0:T(1024)(128)(4,1)}), s8[4194304]{0:T(1024)(128)(4,1)S(1)}, s32[]{:S(2)}) async-start(s8[16777216]{0:T(1024)(128)(4,1)} %bitcast.275), calls=%async_computation.15 | async-start | bytes 8388608 | tf_op jit(solution)/shard_map/while
  1266.5 30.4 %slice-start = ((s8[16777216]{0:T(1024)(128)(4,1)}), s8[4194304]{0:T(1024)(128)(4,1)S(1)}, s32[]{:S(2)}) async-start(s8[16777216]{0:T(1024)(128)(4,1)} %bitcast.275), calls=%async_computation.13 | async-start | bytes 8388608 | tf_op jit(solution)/shard_map/while
  1266.5 30.4 %slice-start.1 = ((s8[16777216]{0:T(1024)(128)(4,1)}), s8[4194304]{0:T(1024)(128)(4,1)S(1)}, s32[]{:S(2)}) async-start(s8[16777216]{0:T(1024)(128)(4,1)} %bitcast.275), calls=%async_computation.14 | async-start | bytes 8388608 | tf_op jit(solution)/shard_map/while
  1266.5 30.4 %slice-start.2 = ((s8[16777216]{0:T(1024)(128)(4,1)}), s8[4194304]{0:T(1024)(128)(4,1)S(1)}, s32[]{:S(2)}) async-start(s8[16777216]{0:T(1024)(128)(4,1)} %bitcast.275), calls=%async_computation.15 | async-start | bytes 8388608 | tf_op jit(solution)/shard_map/while
  1334.6 30.4 %slice-start = ((s8[16777216]{0:T(1024)(128)(4,1)}), s8[4194304]{0:T(1024)(128)(4,1)S(1)}, s32[]{:S(2)}) async-start(s8[16777216]{0:T(1024)(128)(4,1)} %bitcast.275), calls=%async_computation.13 | async-start | bytes 8388608 | tf_op jit(solution)/shard_map/while
  1334.6 30.4 %slice-start.1 = ((s8[16777216]{0:T(1024)(128)(4,1)}), s8[4194304]{0:T(1024)(128)(4,1)S(1)}, s32[]{:S(2)}) async-start(s8[16777216]{0:T(1024)(128)(4,1)} %bitcast.275), calls=%async_computation.14 | async-start | bytes 8388608 | tf_op jit(solution)/shard_map/while
  1334.6 30.4 %slice-start.2 = ((s8[16777216]{0:T(1024)(128)(4,1)}), s8[4194304]{0:T(1024)(128)(4,1)S(1)}, s32[]{:S(2)}) async-start(s8[16777216]{0:T(1024)(128)(4,1)} %bitcast.275), calls=%async_computation.15 | async-start | bytes 8388608 | tf_op jit(solution)/shard_map/while
  1430.6 153.6 %reduce-scatter.5.cloned.1.call-start = ((), (), s32[]{:S(2)}) async-start(), calls=%async_computation.8 | async-start | bytes 3981312 | tf_op jit(solution)/shard_map/reduce_scatter | solution.py:378
  1462.8 16.7 copy-start.43
  1462.8 121.5 %reduce-scatter.9.cloned.1.call-start = ((), (), s32[]{:S(2)}) async-start(), calls=%async_computation.10 | async-start | bytes 5308416 | tf_op jit(solution)/shard_map/reduce_scatter | solution.py:402
  1479.4 154.3 %reduce-scatter.11.cloned.1.call-start = ((), (), s32[]{:S(2)}) async-start(), calls=%async_computation.11 | async-start | bytes 5308416 | tf_op jit(solution)/shard_map/reduce_scatter | solution.py:408
  1479.5 18.9 %copy-start.71 = (bf16[96]{0:T(256)(128)(2,1)S(1)}, bf16[96]{0:T(256)(128)(2,1)}, u32[]{:S(2)}) copy-start(bf16[96]{0:T(256)(128)(2,1)} %param.43) | copy-start | bytes 580
  1495.7 216.3 %all-reduce.25.cloned.1.call-start = ((), (), s32[]{:S(2)}) async-start(), calls=%async_computation.12 | async-start | bytes 3538944 | tf_op jit(solution)/shard_map/psum | solution.py:435
  1522.7 46.2 %copy-start.45 = (f32[2048]{0:T(1024)S(1)}, f32[2048]{0:T(1024)}, u32[]{:S(2)}) copy-start(f32[2048]{0:T(1024)} %copy-done.44) | copy-start | bytes 24580
  (67 other events, 561.0 us)
Sparse Core Ops, SparseCore 0:
  9.9 36.8 all-gather.5
  48.6 23.9 all-gather.7
  74.5 38.7 all-gather.9
  115.0 38.7 all-gather.11
  1430.7 37.0 reduce-scatter.6
  1471.2 47.9 reduce-scatter.4
  1522.6 53.8 reduce-scatter.8
  1580.0 53.7 reduce-scatter.10
  1636.4 75.5 all-reduce.24
where the time goes:
time: 1740 us; the launch traced here: 1730 us
  matrix products  868 us (50%)
  other arithmetic  435 us (25%)
  local copies, waits for them, and re-layouts  147 us (8%)
  waiting for transfers between devices  112 us (6%)
  loops' own time  73.5 us (4%)
  blocking collectives  70.7 us (4%)
  between operations  19.6 us (1%)
    convert_element_type x12, other arithmetic, one_step(): (probabilities * (grad_shares - inner_sum)).astype(jnp.bfloat16)  192 us
    dot_general x24, matrix products, block_scores(): jnp.einsum('qhd,khd->hqk', query_blk, key_blk, preferred_element_type=jnp...  163 us
    dot_general x12, matrix products, one_step(): jnp.einsum('qhd,khd->hqk', grad_blk, value_blk, preferred_element_type=jn...  148 us
    dot_general x12, matrix products, one_step(): jnp.einsum('hqk,qhd->khd', shares, grad_blk, preferred_element_type=jnp.f...  89.8 us
    dot_general x12, matrix products, one_step(): jnp.einsum('hqk,khd->qhd', grad_scores, key_blk, preferred_element_type=j...  89.5 us
    dot_general x12, matrix products, one_step(): jnp.einsum('hqk,qhd->khd', grad_scores, query_blk, preferred_element_type...  83.3 us
    dot_general x12, matrix products, one_piece(): jnp.einsum('hqk,khd->qhd', shares, value_blk, preferred_element_type=jnp....  78.5 us
    dot_general x1, matrix products, on_device(): jnp.dot(normed_two_low, weight_up, preferred_element_type=float32)  68.2 us
  transfers between devices with their start and end apart: 9, of which 2 were waited for; matrix products, arithmetic and copies ran while one was open for 31% of the time, Pallas kernels for 0%

commit v1 on v0

v1 whole, which is shorter than its diff:
```python
import jax
import jax.numpy as jnp
from jax import lax
from jax.experimental import pallas as pl
from jax.experimental.pallas import tpu as pltpu
from jax.sharding import PartitionSpec as P

HEADS = 12
HD = 64
NORM_EPS = 1e-06
LOG2E = 1.4426950408889634
LN2 = 0.6931471805599453
FAR = 512.0
CONST_LANE = 127
BLK = 256
MAX_BLOCKS = 5
VMEM_LIMIT = 60 * 1024 * 1024

F32 = jnp.float32
BF16 = jnp.bfloat16

NT = (((1,), (1,)), ((), ()))
NN = (((1,), (0,)), ((), ()))
TN = (((0,), (0,)), ((), ()))


def dot(lhs, rhs, dims=NN):
    return lax.dot_general(lhs, rhs, dims, preferred_element_type=F32)


def params(**kw):
    return pltpu.CompilerParams(vmem_limit_bytes=VMEM_LIMIT, **kw)


def row_stats(values):
    mean = jnp.mean(values, axis=-1, keepdims=True)
    center = values - mean
    rstd = lax.rsqrt(jnp.mean(center * center, axis=-1, keepdims=True) + NORM_EPS)
    return center * rstd, rstd


def const_spec(shape):
    return pl.BlockSpec(shape, lambda *_: (0,) * len(shape), pipeline_mode=pl.Buffered(1))


def qkv_kernel(x_ref, g_ref, b_ref, w_ref, wb_ref, gq_ref, gk_ref, avg_ref,
               n_ref, q_ref, k_ref, v_ref, rq_ref, rk_ref):
    z, _ = row_stats(x_ref[...].astype(F32))
    normed = (z * g_ref[...] + b_ref[...]).astype(BF16)
    n_ref[...] = normed
    width = q_ref.shape[1]
    avg = avg_ref[...]
    for part in range(3):
        for col in range(0, width, 256):
            at = part * width + col
            pre = dot(normed, w_ref[:, at:at + 256]) + wb_ref[:, at:at + 256]
            if part == 2:
                v_ref[:, col:col + 256] = pre.astype(BF16)
                continue
            high = pre.astype(BF16)
            low = (pre - high.astype(F32)).astype(BF16)
            center = pre - (dot(high, avg) + dot(low, avg))
            rstd = lax.rsqrt(dot((center * center).astype(BF16), avg) + NORM_EPS)
            gain = gk_ref if part else gq_ref
            out = k_ref if part else q_ref
            rout = rk_ref if part else rq_ref
            out[:, col:col + 256] = (center * rstd * gain[:, col:col + 256]).astype(BF16)
            rout[:, col:col + 256] = rstd.astype(BF16)


def qkv_project(x, gain, bias, weight, wbias, gain_q, gain_k, avg):
    total, width = x.shape
    rows = 512
    tile = pl.BlockSpec((rows, width), lambda i: (i, 0))
    outs = [jax.ShapeDtypeStruct((total, width), BF16)] * 6
    return pl.pallas_call(
        qkv_kernel,
        grid=(total // rows,),
        in_specs=[tile, const_spec((1, width)), const_spec((1, width)), const_spec(weight.shape),
                  const_spec((1, 3 * width)), const_spec((1, width)), const_spec((1, width)),
                  const_spec((256, 256))],
        out_specs=[tile] * 6,
        out_shape=outs,
        compiler_params=params(),
        name="qkv_project",
    )(x, gain, bias, weight, wbias, gain_q, gain_k, avg)


def half_masks(rows):
    lane = lax.broadcasted_iota(jnp.int32, (rows, 2 * HD), 1)
    return lane < HD


def for_each_picture(len_ref, off_ref, total, body):
    slots = len_ref.shape[0]

    def one(slot, carry):
        length = len_ref[slot]
        start = off_ref[slot]

        @pl.when(length > 0)
        def _():
            aligned = start // 16 * 16
            count = (start + length - aligned + BLK - 1) // BLK
            for blocks in range(1, MAX_BLOCKS + 1):
                @pl.when(count == blocks)
                def _():
                    first = pl.multiple_of(jnp.minimum(aligned, total - blocks * BLK), 16)
                    body(slot, start, start + length, first, blocks)
        return carry

    lax.fori_loop(0, slots, one, 0)


def inside_rows(first, start, stop, rows, width):
    at = first + lax.broadcasted_iota(jnp.int32, (rows, width), 0)
    return (at >= start) & (at < stop)


def stacked_heads(block, left):
    zero = jnp.zeros_like(block)
    return jnp.concatenate([jnp.where(left, block, zero), jnp.where(left, zero, block)], axis=0)


def slot_lanes(slot, rows):
    lane = lax.broadcasted_iota(jnp.int32, (rows, 128), 1)
    return (lane == slot) | (lane == CONST_LANE)


def fwd_kernel(len_ref, off_ref, q_ref, k_ref, v_ref, aq_ref, ak_ref, o_ref, l_ref):
    total = q_ref.shape[0]
    o_ref[...] = v_ref[...]
    l_ref[...] = jnp.zeros_like(l_ref)
    left = half_masks(BLK)
    one = jnp.ones((BLK, 128), BF16)

    def picture(slot, start, stop, first, blocks):
        span = blocks * BLK
        keys = jnp.concatenate([k_ref[pl.ds(first, span), :], ak_ref[pl.ds(first, span), :]], axis=1)
        vals = v_ref[pl.ds(first, span), :]
        left_all = half_masks(span)
        ones_all = jnp.ones((span, 128), BF16)
        vals = jnp.concatenate([stacked_heads(vals, left_all), stacked_heads(ones_all, left_all)], axis=1)

        def step(j, carry):
            at = pl.multiple_of(first + j * BLK, 16)
            code = jnp.where(slot_lanes(slot, BLK), aq_ref[pl.ds(at, BLK), :], jnp.zeros((), BF16))
            query = stacked_heads(q_ref[pl.ds(at, BLK), :], left)
            query = jnp.concatenate([query, jnp.concatenate([code, code], axis=0)], axis=1)
            shares = jnp.exp2(dot(query, keys, NT)).astype(BF16)
            shares = jnp.concatenate([shares[:BLK], shares[BLK:]], axis=1)
            mixed = dot(shares, vals)
            keep = inside_rows(at, start, stop, BLK, 128)
            inv = 1.0 / mixed[:, 128:]
            o_ref[pl.ds(at, BLK), :] = jnp.where(
                keep, mixed[:, :128] * inv, o_ref[pl.ds(at, BLK), :].astype(F32)).astype(BF16)
            l_ref[pl.ds(at, BLK), :] = jnp.where(keep, inv, l_ref[pl.ds(at, BLK), :])
            return carry

        lax.fori_loop(0, blocks, step, 0)

    for_each_picture(len_ref, off_ref, total, picture)


def attention_forward(lengths, offsets, q, k, v, code_q, code_k):
    total, width = q.shape
    pair = pl.BlockSpec((total, 128), lambda j, *_: (0, j))
    return pl.pallas_call(
        fwd_kernel,
        grid_spec=pltpu.PrefetchScalarGridSpec(
            num_scalar_prefetch=2,
            grid=(width // 128,),
            in_specs=[pair, pair, pair, const_spec((total, 128)), const_spec((total, 128))],
            out_specs=[pair, pair]),
        out_shape=[jax.ShapeDtypeStruct((total, width), BF16), jax.ShapeDtypeStruct((total, width), F32)],
        compiler_params=params(),
        name="attention_forward",
    )(lengths, offsets, q, k, v, code_q, code_k)


def bwd_kernel(len_ref, off_ref, q_ref, k_ref, v_ref, do_ref, da_ref, rq_ref, rk_ref, aq_ref, ak_ref,
               gq_ref, gk_ref, avg_ref,
               oq_ref, ok_ref, ov_ref, dgq_ref, dgk_ref,
               dq_ref, dk_ref, dv_ref, kt_ref, vt_ref):
    total = q_ref.shape[0]
    dq_ref[...] = jnp.zeros_like(dq_ref)
    dk_ref[...] = jnp.zeros_like(dk_ref)
    dv_ref[...] = jnp.zeros_like(dv_ref)
    left = half_masks(BLK)

    def picture(slot, start, stop, first, blocks):
        span = blocks * BLK
        keys_low = k_ref[pl.ds(first, span), :]
        keys = jnp.concatenate([keys_low, ak_ref[pl.ds(first, span), :]], axis=1)
        minus = jnp.full((span, 128), -1.0, BF16)
        vals = jnp.concatenate([v_ref[pl.ds(first, span), :], minus], axis=1)
        keys_st = stacked_heads(keys_low, half_masks(span))
        kt_ref[:, :span] = jnp.zeros((128, span), F32)
        vt_ref[:, :span] = jnp.zeros((128, span), F32)

        def step(j, carry):
            at = pl.multiple_of(first + j * BLK, 16)
            code = jnp.where(slot_lanes(slot, BLK), aq_ref[pl.ds(at, BLK), :], jnp.zeros((), BF16))
            query = stacked_heads(q_ref[pl.ds(at, BLK), :], left)
            grad = stacked_heads(do_ref[pl.ds(at, BLK), :], left)
            delta = stacked_heads(da_ref[pl.ds(at, BLK), :], left)
            weights = jnp.exp2(dot(jnp.concatenate([query, jnp.concatenate([code, code], axis=0)], axis=1), keys, NT))
            slope = dot(jnp.concatenate([grad, delta], axis=1), vals, NT)
            weights_low = weights.astype(BF16)
            scores = (weights * slope).astype(BF16)
            vt_ref[:, :span] += dot(grad, weights_low, TN)
            kt_ref[:, :span] += dot(query, scores, TN)
            wide = jnp.concatenate([scores[:BLK], scores[BLK:]], axis=1)
            new = dot(wide, keys_st)
            keep = inside_rows(at, start, stop, BLK, 128)
            dq_ref[pl.ds(at, BLK), :] = jnp.where(keep, new, dq_ref[pl.ds(at, BLK), :])
            return carry

        lax.fori_loop(0, blocks, step, 0)
        for j in range(blocks):
            at = pl.multiple_of(first + j * BLK, 16)
            keep = inside_rows(at, start, stop, BLK, 128)
            cols = slice(j * BLK, (j + 1) * BLK)
            dk_ref[pl.ds(at, BLK), :] = jnp.where(keep, kt_ref[:, cols].T, dk_ref[pl.ds(at, BLK), :])
            dv_ref[pl.ds(at, BLK), :] = jnp.where(keep, vt_ref[:, cols].T, dv_ref[pl.ds(at, BLK), :])

    for_each_picture(len_ref, off_ref, total, picture)

    avg = avg_ref[...]

    def norm_back(grad, low, gain, unit, rstd):
        z = low.astype(F32) * (1.0 / unit)
        inner = grad * gain
        mean = dot(inner.astype(BF16), avg)
        along = dot((inner * z).astype(BF16), avg)
        return rstd.astype(F32) * (inner - mean - z * along), jnp.sum(grad * z, axis=0, keepdims=True)

    sum_q = jnp.zeros((1, 128), F32)
    sum_k = jnp.zeros((1, 128), F32)
    rows = 512
    for r in range(0, total, rows):
        at = slice(r, r + rows)
        gain_q = gq_ref[...] * HD ** -0.5
        out, part = norm_back(dq_ref[at, :], q_ref[at, :], gain_q, gain_q * LOG2E, rq_ref[at, :])
        oq_ref[at, :] = out.astype(BF16)
        sum_q += part
        gain_k = gk_ref[...]
        out, part = norm_back(dk_ref[at, :] * LN2, k_ref[at, :], gain_k, gain_k, rk_ref[at, :])
        ok_ref[at, :] = out.astype(BF16)
        sum_k += part
        ov_ref[at, :] = dv_ref[at, :].astype(BF16)
    dgq_ref[...] = sum_q * HD ** -0.5
    dgk_ref[...] = sum_k


def attention_backward(lengths, offsets, q, k, v, grad, delta, rstd_q, rstd_k, code_q, code_k, gain_q, gain_k, avg):
    total, width = q.shape
    pair = pl.BlockSpec((total, 128), lambda j, *_: (0, j))
    vec = pl.BlockSpec((1, 128), lambda j, *_: (0, j))
    return pl.pallas_call(
        bwd_kernel,
        grid_spec=pltpu.PrefetchScalarGridSpec(
            num_scalar_prefetch=2,
            grid=(width // 128,),
            in_specs=[pair] * 7 + [const_spec((total, 128))] * 2 + [vec, vec, const_spec((128, 128))],
            out_specs=[pair] * 3 + [vec] * 2,
            scratch_shapes=[pltpu.VMEM((total, 128), F32)] * 3 + [pltpu.VMEM((128, MAX_BLOCKS * BLK), F32)] * 2),
        out_shape=[jax.ShapeDtypeStruct((total, width), BF16)] * 3 + [jax.ShapeDtypeStruct((1, width), F32)] * 2,
        compiler_params=params(),
        name="attention_backward",
    )(lengths, offsets, q, k, v, grad, delta, rstd_q, rstd_k, code_q, code_k, gain_q, gain_k, avg)


def gelu_pair(up):
    density = jnp.exp(-0.5 * (up * up))
    t = 1.0 / (1.0 + (0.3275911 * 0.7071067811865476) * jnp.abs(up))
    poly = 0.5 * 1.061405429
    for coef in (-1.453152027, 1.421413741, -0.284496736, 0.254829592):
        poly = poly * t + 0.5 * coef
    tail = poly * t * density
    return jnp.where(up >= 0, 1.0 - tail, tail), density * 0.3989422804014327


def mlp_kernel(perm_ref, x_ref, c_ref, m_ref, p_ref, l_ref, wo_ref, bo_ref, g2_ref, b2_ref, wu_ref, bu_ref, wd_ref,
               bd_ref, sum_ref,
               out_ref, gh_ref, do_ref, da_ref, dwo_ref, dwu_ref, dwd_ref, dbo_ref, dg2_ref, db2_ref, dbu_ref, dbd_ref,
               awo, awu, awd):
    step = pl.program_id(0)
    parts = perm_ref.shape[0]
    count = pl.num_programs(0) - parts
    width = x_ref.shape[1]
    hidden_width = wu_ref.shape[1]

    @pl.when(step == 0)
    def _():
        for ref in (awo, awu, awd, dbo_ref, dg2_ref, db2_ref, dbu_ref, dbd_ref):
            ref[...] = jnp.zeros(ref.shape, ref.dtype)

    @pl.when(step < count)
    def _():
        mixed = m_ref[...]
        hidden = x_ref[...].astype(F32) + dot(mixed, wo_ref[...]) + bo_ref[...]
        z, rstd = row_stats(hidden)
        normed = (z * g2_ref[...] + b2_ref[...]).astype(BF16)
        grad_out = c_ref[...].astype(F32) * p_ref[...]
        grad_low = grad_out.astype(BF16)
        out = hidden + bd_ref[...]
        grad_norm = jnp.zeros_like(hidden)
        for col in range(0, hidden_width, width):
            cols = slice(col, col + width)
            up = dot(normed, wu_ref[:, cols]) + bu_ref[:, cols]
            grad_act = dot(grad_low, wd_ref[cols, :], NT)
            phi, density = gelu_pair(up)
            act = (up * phi).astype(BF16)
            grad_up = grad_act * (phi + up * density)
            grad_up_low = grad_up.astype(BF16)
            out += dot(act, wd_ref[cols, :])
            awd[cols, :] += dot(act, grad_low, TN)
            awu[:, cols] += dot(normed, grad_up_low, TN)
            grad_norm += dot(grad_up_low, wu_ref[:, cols], NT)
            dbu_ref[:, cols] += jnp.sum(grad_up, axis=0, keepdims=True)
        out_ref[...] = out.astype(BF16)
        dbd_ref[...] += jnp.sum(grad_out, axis=0, keepdims=True)
        dg2_ref[...] += jnp.sum(grad_norm * z, axis=0, keepdims=True)
        db2_ref[...] += jnp.sum(grad_norm, axis=0, keepdims=True)
        inner = grad_norm * g2_ref[...]
        grad_hidden = grad_out + rstd * (inner - jnp.mean(inner, axis=-1, keepdims=True)
                                         - z * jnp.mean(inner * z, axis=-1, keepdims=True))
        gh_ref[...] = grad_hidden
        branch = grad_hidden.astype(BF16)
        dbo_ref[...] += jnp.sum(grad_hidden, axis=0, keepdims=True)
        awo[...] += dot(mixed, branch, TN)
        grad_mixed = dot(branch, wo_ref[...], NT)
        inv = l_ref[...]
        scaled = grad_mixed * inv
        do_ref[...] = scaled.astype(BF16)
        prod = scaled * mixed.astype(F32)
        high = prod.astype(BF16)
        low = (prod - high.astype(F32)).astype(BF16)
        lane = lax.broadcasted_iota(jnp.int32, (prod.shape[0], 256), 1) % HD
        for col in range(0, width, 256):
            cols = slice(col, col + 256)
            delta = dot(high[:, cols], sum_ref[...]) + dot(low[:, cols], sum_ref[...])
            first = delta.astype(BF16)
            rest = delta - first.astype(F32)
            da_ref[:, cols] = jnp.where(lane == 0, first.astype(F32), jnp.where(lane == 1, rest, 0.0)).astype(BF16)

    @pl.when(step >= count)
    def _():
        part = perm_ref[jnp.maximum(step - count, 0)]
        for acc, ref in ((awo, dwo_ref), (awu, dwu_ref), (awd, dwd_ref)):
            rows = ref.shape[0]
            ref[...] = acc[pl.ds(pl.multiple_of(part * rows, 16), rows), :].astype(BF16)


def mlp_both(perm, x, cot, mixed, pad, linv, wo, bo, g2, b2, wu, bu, wd, bd, summer):
    total, width = x.shape
    ff = wu.shape[1]
    parts = perm.shape[0]
    rows = 256
    count = total // rows
    tile = pl.BlockSpec((rows, width), lambda i, *_: (jnp.minimum(i, count - 1), 0))

    def grad_spec(shape):
        return pl.BlockSpec((shape[0] // parts, shape[1]), lambda i, *_: (jnp.maximum(i - count, 0), 0))

    vec = pl.BlockSpec((1, width), lambda i, *_: (0, 0))
    vec_ff = pl.BlockSpec((1, ff), lambda i, *_: (0, 0))
    return pl.pallas_call(
        mlp_kernel,
        grid_spec=pltpu.PrefetchScalarGridSpec(
            num_scalar_prefetch=1,
            grid=(count + parts,),
            in_specs=[tile, tile, tile, pl.BlockSpec((rows, 1), lambda i, *_: (jnp.minimum(i, count - 1), 0)), tile,
                      const_spec(wo.shape), const_spec((1, width)), const_spec((1, width)), const_spec((1, width)),
                      const_spec(wu.shape), const_spec((1, ff)), const_spec(wd.shape), const_spec((1, width)),
                      const_spec((256, 256))],
            out_specs=[tile, tile, tile, tile, grad_spec(wo.shape), grad_spec(wu.shape), grad_spec(wd.shape),
                       vec, vec, vec, vec_ff, vec],
            scratch_shapes=[pltpu.VMEM(wo.shape, F32), pltpu.VMEM(wu.shape, F32), pltpu.VMEM(wd.shape, F32)]),
        out_shape=[jax.ShapeDtypeStruct((total, width), BF16), jax.ShapeDtypeStruct((total, width), F32),
                   jax.ShapeDtypeStruct((total, width), BF16), jax.ShapeDtypeStruct((total, width), BF16),
                   jax.ShapeDtypeStruct(wo.shape, BF16), jax.ShapeDtypeStruct(wu.shape, BF16),
                   jax.ShapeDtypeStruct(wd.shape, BF16)]
        + [jax.ShapeDtypeStruct((1, n), F32) for n in (width, width, width, ff, width)],
        compiler_params=params(),
        name="mlp_both",
    )(perm, x, cot, mixed, pad, linv, wo, bo, g2, b2, wu, bu, wd, bd, summer)


def dqkv_kernel(perm_ref, n_ref, gq_ref, gk_ref, gv_ref, dw_ref, db_ref, acc):
    parts = perm_ref.shape[0]
    total, width = n_ref.shape
    rows = width // parts
    ones = jnp.ones((8, total), BF16)
    for i, ref in enumerate((gq_ref, gk_ref, gv_ref)):
        @pl.when(pl.program_id(0) == i)
        def _():
            acc[...] = dot(n_ref[...], ref[...], TN)
            db_ref[...] = dot(ones, ref[...])[:1]
    for part in range(parts):
        dw_ref[part * rows:(part + 1) * rows, :] = acc[
            pl.ds(pl.multiple_of(perm_ref[part] * rows, 8), rows), :].astype(BF16)


def qkv_weight_grad(perm, normed, gq, gk, gv):
    total, width = normed.shape
    return pl.pallas_call(
        dqkv_kernel,
        grid_spec=pltpu.PrefetchScalarGridSpec(
            num_scalar_prefetch=1,
            grid=(3,),
            in_specs=[const_spec((total, width))] * 4,
            out_specs=[pl.BlockSpec((width, width), lambda i, *_: (0, i)), pl.BlockSpec((1, width), lambda i, *_: (0, i))],
            scratch_shapes=[pltpu.VMEM((width, width), F32)]),
        out_shape=[jax.ShapeDtypeStruct((width, 3 * width), BF16), jax.ShapeDtypeStruct((1, 3 * width), F32)],
        compiler_params=params(),
        name="qkv_weight_grad",
    )(perm, normed, gq, gk, gv)


def dinput_kernel(x_ref, gh_ref, gq_ref, gk_ref, gv_ref, w_ref, g_ref, out_ref, dg_ref, db_ref):
    width = x_ref.shape[1]

    @pl.when(pl.program_id(0) == 0)
    def _():
        dg_ref[...] = jnp.zeros_like(dg_ref)
        db_ref[...] = jnp.zeros_like(db_ref)

    grad = dot(gq_ref[...], w_ref[:, :width], NT)
    grad += dot(gk_ref[...], w_ref[:, width:2 * width], NT)
    grad += dot(gv_ref[...], w_ref[:, 2 * width:], NT)
    z, rstd = row_stats(x_ref[...].astype(F32))
    dg_ref[...] += jnp.sum(grad * z, axis=0, keepdims=True)
    db_ref[...] += jnp.sum(grad, axis=0, keepdims=True)
    inner = grad * g_ref[...]
    out_ref[...] = gh_ref[...] + rstd * (inner - jnp.mean(inner, axis=-1, keepdims=True)
                                         - z * jnp.mean(inner * z, axis=-1, keepdims=True))


def input_grad(x, gh, gq, gk, gv, weight, gain):
    total, width = x.shape
    rows = 512
    tile = pl.BlockSpec((rows, width), lambda i: (i, 0))
    vec = pl.BlockSpec((1, width), lambda i: (0, 0))
    return pl.pallas_call(
        dinput_kernel,
        grid=(total // rows,),
        in_specs=[tile] * 5 + [const_spec(weight.shape), const_spec((1, width))],
        out_specs=[tile, vec, vec],
        out_shape=[jax.ShapeDtypeStruct((total, width), F32)] + [jax.ShapeDtypeStruct((1, width), F32)] * 2,
        compiler_params=params(),
        name="input_grad",
    )(x, gh, gq, gk, gv, weight, gain)


def gather(block):
    return lax.all_gather(block, "shard", axis=0, tiled=True)


def reduce_owned(grad):
    own = lax.psum_scatter(grad, "shard", scatter_dimension=0, tiled=True)
    return lax.psum(own, "rep").astype(F32)


PARTS = 8


def block_order():
    return jnp.arange(PARTS, dtype=jnp.int32)


def on_device(shards, reps, inputs, cotangent, picture_ids, picture_lengths, picture_offsets, padding, ln1_gain,
              ln1_bias, qkv_weight, qkv_bias, query_gain, key_gain, out_weight, out_bias, ln2_gain, ln2_bias,
              up_weight, up_bias, down_weight, down_bias):
    total, width = inputs.shape
    pairs = width // 128
    small = (ln1_gain, ln1_bias, qkv_bias, query_gain, key_gain, out_bias, ln2_gain, ln2_bias, up_bias, down_bias)
    sizes = [a.shape[0] for a in small]
    packed = gather(jnp.concatenate(small)[None])
    at = 0
    full = []
    for size in sizes:
        full.append(packed[:, at:at + size].reshape(1, shards * size).astype(F32))
        at += size
    gain_one, shift_one, bias_qkv, gain_query, gain_key, bias_out, gain_two, shift_two, bias_up, bias_down = full
    weight_qkv = gather(qkv_weight)
    weight_out = gather(out_weight)
    weight_up = gather(up_weight)
    weight_down = gather(down_weight)

    lengths = picture_lengths.reshape(-1)
    offsets = picture_offsets.reshape(-1)
    live = padding > 0
    lane = jnp.arange(128, dtype=jnp.int32)[None]
    held = ((picture_ids[:, None] == lane) & live[:, None]).astype(F32)
    last = (lane == CONST_LANE).astype(F32)
    code_q = (held + last).astype(BF16)
    code_k = ((held - last) * FAR).astype(BF16)
    head = jnp.arange(256, dtype=jnp.int32) // HD
    summer = (head[:, None] == head[None]).astype(BF16)
    avg = (summer.astype(F32) * (1.0 / HD)).astype(BF16)
    gain_q = jnp.tile(gain_query, (1, HEADS))
    gain_k = jnp.tile(gain_key, (1, HEADS))

    normed, q, k, v, rstd_q, rstd_k = qkv_project(
        inputs, gain_one, shift_one, weight_qkv, bias_qkv, gain_q * (HD ** -0.5 * LOG2E), gain_k, avg)
    mixed, linv = attention_forward(lengths, offsets, q, k, v, code_q, code_k)
    perm = block_order()
    (output, grad_hidden, grad_scaled, delta, dwo, dwu, dwd, dbo, dg2, db2, dbu, dbd) = mlp_both(
        perm, inputs, cotangent, mixed, padding.astype(F32)[:, None], linv, weight_out, bias_out, gain_two, shift_two,
        weight_up, bias_up, weight_down, bias_down, summer)
    own_down = reduce_owned(dwd)
    own_up = reduce_owned(dwu)
    own_out = reduce_owned(dwo)
    gq, gk, gv, dgq, dgk = attention_backward(
        lengths, offsets, q, k, v, grad_scaled, delta, rstd_q, rstd_k, code_q, code_k, gain_q, gain_k,
        avg[:128, :128])
    dw, db = qkv_weight_grad(perm, normed, gq, gk, gv)
    own_qkv = reduce_owned(dw)
    grad_input, dg1, db1 = input_grad(inputs, grad_hidden, gq, gk, gv, weight_qkv, gain_one)
    dgq = jnp.sum(dgq.reshape(HEADS, HD), axis=0)
    dgk = jnp.sum(dgk.reshape(HEADS, HD), axis=0)
    vectors = (dg1, db1, db, dgq, dgk, dbo, dg2, db2, dbu, dbd)
    rows = jnp.concatenate([g.reshape(shards, -1) for g in vectors], axis=1)
    own = reduce_owned(rows)[0]
    at = 0
    owned = []
    for size in sizes:
        owned.append(own[at:at + size])
        at += size
    og1, ob1, obqkv, ogq, ogk, obo, og2, ob2, obu, obd = owned
    return (output, grad_input, og1, ob1, own_qkv, obqkv, ogq, ogk, own_out, obo, og2, ob2, own_up, obu, own_down, obd)


def solution(mesh):
    rows2 = P(("rep", "shard"), None)
    rows1 = P(("rep", "shard"))
    vec, mat = P("shard"), P("shard", None)
    in_specs = (rows2, rows2, rows1, rows2, rows2, rows1, vec, vec, mat, vec, vec, vec, mat, vec, vec, vec, mat, vec,
                mat, vec)
    out_specs = (rows2, rows2, vec, vec, mat, vec, vec, vec, mat, vec, vec, vec, mat, vec, mat, vec)
    shards, reps = mesh.shape["shard"], mesh.shape["rep"]

    def body(*args):
        return on_device(shards, reps, *args)

    return jax.shard_map(body, mesh=mesh, in_specs=in_specs, out_specs=out_specs, check_vma=False)
```

time: 1740 us -> 636 us (0.37)
  matrix products: 868 us -> 0 us
  other arithmetic: 435 us -> 14.7 us
  Pallas kernels: 0 us -> 274 us
  local copies, waits for them, and re-layouts: 147 us -> 23.1 us
  waiting for transfers between devices: 112 us -> 235 us
  loops' own time: 73.5 us -> 0 us
    dot_general x96 -> x0, matrix products: 868 us -> none  [the longest x24 163 us: block_scores(): jnp.einsum('qhd,khd->hqk', query_blk, key_blk, preferred_element_type=jnp...]
    pallas_call x0 -> x6, Pallas kernels: none -> 274 us  [the longest x1 104 us: mlp_both(): pl.pallas_call(mlp_kernel, grid_spec=pltpu.PrefetchScalarGridSpec(num_sca...]
    convert_element_type x39 -> x12, other arithmetic: 221 us -> 11.8 us  [the longest x4 6.95 us: reduce_owned(): return lax.psum(own, 'rep').astype(F32)]
    reduce_scatter x4, waiting for transfers between devices: 49.5 us -> 184 us  [reduce_owned(): own = lax.psum_scatter(grad, 'shard', scatter_dimension=0, tiled=True)]
    reduce_sum x27 -> x2, other arithmetic: 118 us -> 0.05 us  [the longest x1 0.02 us: on_device(): dgq = jnp.sum(dgq.reshape(HEADS, HD), axis=0)]
    another operation x2 -> x0, loops' own time: 73.5 us -> none  [the longest x1 48.4 us: attention_backward(): lax.scan(one_step, (zeros_all, zeros_all), counters)]
    or x24 -> x0, other arithmetic: 64.4 us -> none  [allowed_block(): return inside & living | (key_pos[None, :] == query_pos[:, None])]
    psum x1, waiting for transfers between devices: 60.1 us -> 18.3 us  [reduce_owned(): return lax.psum(own, 'rep').astype(F32)]
  transfers between devices with their start and end apart: 9 -> 9, of which waited for: 2 -> 5; matrix products, arithmetic and copies ran while one was open for 31% -> 5% of each run, Pallas kernels for 0% -> 27%
where the time goes in v1:
time: 636 us; the launch traced here: 625 us
  Pallas kernels  274 us (43%)
  waiting for transfers between devices  235 us (37%)
  blocking collectives  63.5 us (10%)
  local copies, waits for them, and re-layouts  23.1 us (4%)
  between operations  15.2 us (2%)
  other arithmetic  14.7 us (2%)
    reduce_scatter x4, waiting for transfers between devices, reduce_owned(): own = lax.psum_scatter(grad, 'shard', scatter_dimension=0, tiled=True)  184 us
    pallas_call x1, Pallas kernels, mlp_both(): pl.pallas_call(mlp_kernel, grid_spec=pltpu.PrefetchScalarGridSpec(num_sca...  104 us
    pallas_call x1, Pallas kernels, attention_backward(): pl.pallas_call(bwd_kernel, grid_spec=pltpu.PrefetchScalarGridSpec(num_sca...  70.1 us
    unnamed x2, blocking collectives  50.9 us
    pallas_call x1, Pallas kernels, attention_forward(): pl.pallas_call(fwd_kernel, grid_spec=pltpu.PrefetchScalarGridSpec(num_sca...  48.8 us
    all_gather x4, waiting for transfers between devices, gather(): return lax.all_gather(block, 'shard', axis=0, tiled=True)  28.1 us
    pallas_call x1, Pallas kernels, qkv_project(): pl.pallas_call(qkv_kernel, grid=(total // rows,), in_specs=[tile, const_s...  18.3 us
    psum x1, waiting for transfers between devices, reduce_owned(): return lax.psum(own, 'rep').astype(F32)  18.3 us
  transfers between devices with their start and end apart: 9, of which 5 were waited for; matrix products, arithmetic and copies ran while one was open for 5% of the time, Pallas kernels for 27%

profile of v1, /device:TPU:0, one launch (start us, length us, event | category | flops | bytes accessed | tf_op | source)
XLA Modules:
  0.0 625.2 jit_solution(12656117151729646527)
XLA Ops:
  7.2 0.7 all-gather.6.cloned.1.call-update
  8.0 0.7 all-gather.8.cloned.1.call-update
  8.7 0.7 all-gather.10.cloned.1.call-update
  9.5 0.5 all-gather.12.cloned.1.call-update
  10.1 0.7 convert_element_type.132
  10.8 1.3 fusion.4
  12.7 6.8 %concatenate.6 = bf16[1264]{0:T(1024)(128)(2,1)S(1)} concatenate(bf16[96]{0:T(256)(128)(2,1)} %param.26, bf16[96]{0:T(256)(128)(2,1)} %param.27, bf16[288]{0:T(512)(128)(2,1)} %param.29, bf16[8]{0:T(256)(128)(2,1)} %param.30, bf16[8]{0:T(256)(128)(2,1)} %param.31, bf16[96]{0:T(256)(128)(2,1)} %param.33, bf16[96]{0:T(256)(128)(2,1)} %param.34, bf16[96]{0:T(256)(128)(2,1)} %param.35, ...), dimensions={0} | concatenate | bytes 5056 | tf_op jit(solution)/shard_map/concatenate | solution.py:480
  19.6 0.3 dynamic-update-slice
  19.8 26.4 %all-reduce = bf16[10112]{0:T(1024)(128)(2,1)S(1)} all-reduce(bf16[10112]{0:T(1024)(128)(2,1)S(1)} %dynamic-update-slice), channel_id=2, replica_groups=mesh['rep'=4,'shard'=8] {'shard'}, use_global_device_ids=true, to_apply=%add | all-reduce | flops 10112 | bytes 40448
  46.2 0.1 reshape.310
  46.3 0.1 slice_convert_fusion.5
  46.4 0.1 reshape.304
  46.5 0.1 reshape.303
  46.6 0.1 tile.9.gq_ref
  46.6 0.7 tile.21.gk_ref
  47.4 0.7 reshape.302.wb_ref
  48.1 0.6 copy.38
  48.8 0.1 slice_convert_fusion.1
  48.8 0.7 reshape.309.bd_ref
  49.5 0.7 reshape.300.g_ref
  50.2 0.7 reshape.307.b2_ref
  50.8 0.7 reshape.306.g2_ref
  51.5 0.7 reshape.305.bo_ref
  52.2 0.7 reshape.301.b_ref
  52.8 1.3 copy.37.p_ref
  54.2 0.6 broadcast_multiply_fusion.gq_ref
  54.8 0.8 multiply_convert_fusion.avg_ref
  55.5 0.7 compare_convert_fusion.sum_ref
  56.3 2.4 fusion.2
  58.7 18.3 %qkv_project.1 = (bf16[2048,768]{1,0:T(8,128)(2,1)}, bf16[2048,768]{1,0:T(8,128)(2,1)}, bf16[2048,768]{1,0:T(8,128)(2,1)}, bf16[2048,768]{1,0:T(8,128)(2,1)}, bf...) custom-call(bf16[2048,768]{1,0:T(8,128)(2,1)} %x_ref.5, f32[1,768]{1,0:T(1,128)} %reshape.300.g_ref, ...), custom_call_target="tpu_custom_call" | custom-call | tf_op jit(solution)/shard_map/qkv_project/pallas_call | solution.py:76
  77.0 48.8 %attention_forward.1 = (bf16[2048,768]{1,0:T(8,128)(2,1)}, f32[2048,768]{1,0:T(8,128)}) custom-call(s32[20]{0:T(128)} %bitcast.27, s32[20]{0:T(128)} %bitcast.29, bf16[2048,768]{1,0:T(8,128)(2,1)} %get-tuple-element.46.q_ref, bf16[2048,768]{1,0:T(8,128)(2,1)} %get-tuple-element.47.k_ref, bf16[2048,768]{1,0:T(8,128)(2,1)} %get-tuple-element.48.v_ref, ...), custom_call_target="tpu_custom_call" | custom-call | tf_op jit(solution)/shard_map/attention_forward/pallas_call | solution.py:168
  125.9 28.1 %all-gather.12.cloned.1.call-done.wd_ref = bf16[3072,768]{1,0:T(8,128)(2,1)} async-done(((bf16[384,768]{1,0:T(8,128)(2,1)}), bf16[3072,768]{1,0:T(8,128)(2,1)}) %all-gather.12.cloned.1.call-update) | async-done | bytes 4718608 | tf_op jit(solution)/shard_map/all_gather | solution.py:458
  153.9 0.5 iota.25.perm_ref
  154.5 104.1 %mlp_both.1 = (bf16[2048,768]{1,0:T(8,128)(2,1)}, f32[2048,768]{1,0:T(8,128)}, bf16[2048,768]{1,0:T(8,128)(2,1)}, bf16[2048,768]{1,0:T(8,128)(2,1)}, bf16[768,76...) custom-call(s32[8]{0:T(128)} %iota.25.perm_ref, ...), custom_call_target="tpu_custom_call" | custom-call | tf_op jit(solution)/shard_map/mlp_both/pallas_call | solution.py:369
  258.7 1.4 slice.134.avg_ref
  260.1 70.1 %attention_backward.1 = (bf16[2048,768]{1,0:T(8,128)(2,1)}, bf16[2048,768]{1,0:T(8,128)(2,1)}, bf16[2048,768]{1,0:T(8,128)(2,1)}, f32[1,768]{1,0:T(1,128)}, f32[1,768]{1,0:T(1,128)}) custom-call(s32[20]{0:T(128)} %bitcast.28, s32[20]{0:T(128)} %bitcast.30, bf16[2048,768]{1,0:T(8,128)(2,1)} %get-tuple-element.46.q_ref, ...), custom_call_target="tpu_custom_call" | custom-call | tf_op jit(solution)/shard_map/attention_backward/pallas_call | solution.py:260
  330.1 0.5 iota.28.perm_ref
  330.7 16.1 %qkv_weight_grad.1 = (bf16[768,2304]{1,0:T(8,128)(2,1)}, f32[1,2304]{1,0:T(1,128)}) custom-call(s32[8]{0:T(128)} %iota.28.perm_ref, bf16[2048,768]{1,0:T(8,128)(2,1)} %get-tuple-element.63.n_ref, bf16[2048,768]{1,0:T(8,128)(2,1)} %get-tuple-element.57.gq_ref, bf16[2048,768]{1,0:T(8,128)(2,1)} %get-tuple-element.58.gk_ref, ...), custom_call_target="tpu_custom_call" | custom-call | tf_op jit(solution)/shard_map/qkv_weight_grad/pallas_call | solution.py:408
  346.9 0.7 reduce-scatter.9.cloned.1.call-update
  347.7 0.6 reduce-scatter.11.cloned.1.call-update
  348.4 69.8 %reduce-scatter.5.cloned.1.call-done = bf16[96,2304]{1,0:T(8,128)(2,1)} async-done(((bf16[768,2304]{1,0:T(8,128)(2,1)}), bf16[96,2304]{1,0:T(8,128)(2,1)}) %reduce-scatter.5.cloned.1.call-update) | async-done | bytes 442384 | tf_op jit(solution)/shard_map/reduce_scatter | solution.py:462
  418.2 57.3 %reduce-scatter.9.cloned.1.call-done = bf16[96,3072]{1,0:T(8,128)(2,1)} async-done(((bf16[768,3072]{1,0:T(8,128)(2,1)}), bf16[96,3072]{1,0:T(8,128)(2,1)}) %reduce-scatter.9.cloned.1.call-update) | async-done | bytes 589840 | tf_op jit(solution)/shard_map/reduce_scatter | solution.py:462
  475.5 57.2 %reduce-scatter.11.cloned.1.call-done = bf16[384,768]{1,0:T(8,128)(2,1)} async-done(((bf16[3072,768]{1,0:T(8,128)(2,1)}), bf16[384,768]{1,0:T(8,128)(2,1)}) %reduce-scatter.11.cloned.1.call-update) | async-done | bytes 589840 | tf_op jit(solution)/shard_map/reduce_scatter | solution.py:462
  532.9 0.1 reshape.292
  533.1 0.1 reshape.294
  533.5 0.5 broadcast.91
  534.0 0.7 reduce.16
  534.8 0.1 reshape.290
  534.9 16.2 %input_grad.1 = (f32[2048,768]{1,0:T(8,128)}, f32[1,768]{1,0:T(1,128)}, f32[1,768]{1,0:T(1,128)}) custom-call(bf16[2048,768]{1,0:T(8,128)(2,1)} %x_ref.5, f32[2048,768]{1,0:T(8,128)} %get-tuple-element.52.gh_ref, bf16[2048,768]{1,0:T(8,128)(2,1)} %get-tuple-element.57.gq_ref, bf16[2048,768]{1,0:T(8,128)(2,1)} %get-tuple-element.58.gk_ref, ...), custom_call_target="tpu_custom_call" | custom-call | tf_op jit(solution)/shard_map/input_grad/pallas_call | solution.py:446
  551.0 0.7 reduce
  551.8 0.7 reduce.1
  552.6 0.1 concatenate.7
  552.7 24.6 %all-reduce.1 = f32[8,1264]{1,0:T(8,128)S(1)} all-reduce(f32[8,1264]{1,0:T(8,128)S(1)} %concatenate.7), channel_id=3, replica_groups=mesh['rep'=4,'shard'=8] {'shard'}, use_global_device_ids=true, to_apply=%region_2.3.clone | all-reduce | flops 10112 | bytes 80896
  577.2 0.7 constant_dynamic-slice_fusion
  577.9 12.6 %psum.35 = f32[1,1264]{1,0:T(1,128)S(1)} all-reduce(f32[1,1264]{1,0:T(1,128)S(1)} %constant_dynamic-slice_fusion), channel_id=1, replica_groups=mesh['rep'=4,'shard'=8] {'rep'}, use_global_device_ids=true, to_apply=%region_3.4 | all-reduce | flops 1264 | bytes 10112 | tf_op jit(solution)/shard_map/psum | solution.py:463
  590.5 0.7 slice_reduce_fusion.1
  591.2 0.7 slice_reduce_fusion
  591.8 0.6 slice_bitcast_fusion.4
  592.4 0.6 slice_bitcast_fusion
  593.0 18.3 %all-reduce.5.cloned.1.call-done = (bf16[96,2304]{1,0:T(8,128)(2,1)}, bf16[96,768]{1,0:T(8,128)(2,1)}, bf16[96,3072]{1,0:T(8,128)(2,1)}, bf16[384,768]{1,0:T(8,128)(2,1)}) async-done(((bf16[96,2304]{1,0:T(8,128)(2,1)}, bf16[96,768]{1,0:T(8,128)(2,1)}, bf16[96,3072]{1,0:T(8,128)(2,1)}, bf16[384,768]{1,0:T(8,128)(2,1)}), (bf16[96,2304]{1,0:T(8,128)(2,1)}, bf16[96,768]{1,0:T(8,128)(2,1)}, ...) | async-done | bytes 1769488 | tf_op jit(solution)/shard_map/psum | solution.py:463
  611.3 1.7 convert_element_type.144
  613.0 2.0 convert_element_type.143
  615.0 2.2 convert_element_type.145
  617.2 1.1 convert_element_type.146
  (66 shorter events, 1.4 us)
Async XLA Ops:
  7.2 47.6 %copy-start.1 = (s32[2048]{0:T(1024)S(1)}, s32[2048]{0:T(1024)}, u32[]{:S(2)}) copy-start(s32[2048]{0:T(1024)} %param.25) | copy-start | bytes 24580
  7.2 49.1 %copy-start.5 = (s32[2048]{0:T(1024)S(1)}, s32[2048]{0:T(1024)}, u32[]{:S(2)}) copy-start(s32[2048]{0:T(1024)} %param.22) | copy-start | bytes 24580
  7.2 51.5 %all-gather.6.cloned.1.call-start = ((), (), s32[]{:S(2)}) async-start(), calls=%async_computation.4 | async-start | bytes 3981312 | tf_op jit(solution)/shard_map/all_gather | solution.py:458
  7.9 117.9 %all-gather.8.cloned.1.call-start = ((), (), s32[]{:S(2)}) async-start(), calls=%async_computation.5 | async-start | bytes 1327104 | tf_op jit(solution)/shard_map/all_gather | solution.py:458
  8.7 117.2 %all-gather.10.cloned.1.call-start = ((), (), s32[]{:S(2)}) async-start(), calls=%async_computation.6 | async-start | bytes 5308416 | tf_op jit(solution)/shard_map/all_gather | solution.py:458
  9.4 144.5 %all-gather.12.cloned.1.call-start = ((), (), s32[]{:S(2)}) async-start(), calls=%async_computation.7 | async-start | bytes 5308416 | tf_op jit(solution)/shard_map/all_gather | solution.py:458
  10.0 338.4 %reduce-scatter.7.cloned.1.call-start = ((), (), s32[]{:S(2)}) async-start(), calls=%async_computation.9 | async-start | bytes 1327104 | tf_op jit(solution)/shard_map/reduce_scatter | solution.py:462
  46.6 30.4 %copy-start.2 = (f32[1,768]{1,0:T(1,128)}, f32[1,768]{1,0:T(1,128)S(1)}, u32[]{:S(2)}) copy-start(f32[1,768]{1,0:T(1,128)S(1)} %tile.9.gq_ref) | copy-start | bytes 9220
  258.6 159.6 %reduce-scatter.5.cloned.1.call-start = ((), (), s32[]{:S(2)}) async-start(), calls=%async_computation.8 | async-start | bytes 3981312 | tf_op jit(solution)/shard_map/reduce_scatter | solution.py:462
  346.8 128.7 %reduce-scatter.9.cloned.1.call-start = ((), (), s32[]{:S(2)}) async-start(), calls=%async_computation.10 | async-start | bytes 5308416 | tf_op jit(solution)/shard_map/reduce_scatter | solution.py:462
  347.6 185.2 %reduce-scatter.11.cloned.1.call-start = ((), (), s32[]{:S(2)}) async-start(), calls=%async_computation.11 | async-start | bytes 5308416 | tf_op jit(solution)/shard_map/reduce_scatter | solution.py:462
  347.6 185.1 %copy-start.11 = (f32[1,768]{1,0:T(1,128)S(1)}, f32[1,768]{1,0:T(1,128)}, u32[]{:S(2)}) copy-start(f32[1,768]{1,0:T(1,128)} %get-tuple-element.65) | copy-start | bytes 9220
  347.6 185.3 %copy-start.10 = (f32[1,768]{1,0:T(1,128)S(1)}, f32[1,768]{1,0:T(1,128)}, u32[]{:S(2)}) copy-start(f32[1,768]{1,0:T(1,128)} %get-tuple-element.66) | copy-start | bytes 9220
  347.6 185.5 %copy-start.9 = (f32[1,768]{1,0:T(1,128)S(1)}, f32[1,768]{1,0:T(1,128)}, u32[]{:S(2)}) copy-start(f32[1,768]{1,0:T(1,128)} %get-tuple-element.67) | copy-start | bytes 9220
  347.6 185.6 %copy-start.8 = (f32[1,768]{1,0:T(1,128)S(1)}, f32[1,768]{1,0:T(1,128)}, u32[]{:S(2)}) copy-start(f32[1,768]{1,0:T(1,128)} %get-tuple-element.68) | copy-start | bytes 9220
  347.6 185.7 %copy-start.7 = (f32[1,768]{1,0:T(1,128)S(1)}, f32[1,768]{1,0:T(1,128)}, u32[]{:S(2)}) copy-start(f32[1,768]{1,0:T(1,128)} %get-tuple-element.69) | copy-start | bytes 9220
  347.7 185.8 %copy-start.6 = (f32[1,768]{1,0:T(1,128)S(1)}, f32[1,768]{1,0:T(1,128)}, u32[]{:S(2)}) copy-start(f32[1,768]{1,0:T(1,128)} %get-tuple-element.71) | copy-start | bytes 9220
  347.7 186.4 %copy-start.3 = (f32[1,3072]{1,0:T(1,128)S(1)}, f32[1,3072]{1,0:T(1,128)}, u32[]{:S(2)}) copy-start(f32[1,3072]{1,0:T(1,128)} %get-tuple-element.70) | copy-start | bytes 36868
  347.7 187.1 %copy-start.4 = (f32[1,2304]{1,0:T(1,128)S(1)}, f32[1,2304]{1,0:T(1,128)}, u32[]{:S(2)}) copy-start(f32[1,2304]{1,0:T(1,128)} %get-tuple-element.64) | copy-start | bytes 27652
  348.3 263.0 %all-reduce.5.cloned.1.call-start = ((), (), s32[]{:S(2)}) async-start(), calls=%async_computation.12 | async-start | bytes 3538944 | tf_op jit(solution)/shard_map/psum | solution.py:463
  611.3 5.9 copy-start
Sparse Core Ops, SparseCore 0:
  9.9 36.7 all-gather.5
  48.5 23.9 all-gather.7
  74.4 38.7 all-gather.9
  115.0 38.9 all-gather.11
  258.8 36.6 reduce-scatter.6
  346.9 71.2 reduce-scatter.4
  421.7 53.7 reduce-scatter.8
  478.9 53.7 reduce-scatter.10
  535.4 75.8 all-reduce.4

commit v2 on v1

--- a/solution.py
+++ b/solution.py
@@ -1,9 +1,12 @@
+import functools
+
 import jax
 import jax.numpy as jnp
 from jax import lax
 from jax.experimental import pallas as pl
 from jax.experimental.pallas import tpu as pltpu
 from jax.sharding import PartitionSpec as P
+
 
 HEADS = 12
 HD = 64
@@ -15,6 +18,8 @@
 BLK = 256
 MAX_BLOCKS = 5
 VMEM_LIMIT = 60 * 1024 * 1024
+PARTS = 8
+SMALL = 16
 
 F32 = jnp.float32
 BF16 = jnp.bfloat16
@@ -30,6 +35,10 @@
 
 def params(**kw):
     return pltpu.CompilerParams(vmem_limit_bytes=VMEM_LIMIT, **kw)
+
+
+def cost(flops, traffic):
+    return pl.CostEstimate(flops=int(flops), transcendentals=0, bytes_accessed=int(traffic))
 
 
 def row_stats(values):
@@ -43,47 +52,85 @@
     return pl.BlockSpec(shape, lambda *_: (0,) * len(shape), pipeline_mode=pl.Buffered(1))
 
 
-def qkv_kernel(x_ref, g_ref, b_ref, w_ref, wb_ref, gq_ref, gk_ref, avg_ref,
-               n_ref, q_ref, k_ref, v_ref, rq_ref, rk_ref):
+def any_specs(count):
+    return [pl.BlockSpec(memory_space=pl.ANY)] * count
+
+
+class Laid:
+    def __init__(self, pieces, coded):
+        self.pieces, self.coded = pieces, coded
+
+    def start(self, own, refs, dst, sem):
+        for which, row, rows, place, col in self.pieces:
+            ref = refs[which]
+            if rows is None:
+                pltpu.make_async_copy(ref, dst, sem).start()
+                continue
+            at = pl.multiple_of((own ^ place) * rows, 16) if self.coded else place * rows
+            width = ref.shape[1]
+            pltpu.make_async_copy(ref.at[pl.ds(row, rows), :],
+                                  dst.at[pl.ds(at, rows), pl.ds(col * width, width)], sem).start()
+
+    def wait(self, dst, sem):
+        pltpu.make_async_copy(dst, dst, sem).wait()
+
+
+def qkv_kernel(own_ref, *refs, count, laid):
+    block_refs, refs = refs[:count], refs[count:]
+    (x_ref, g_ref, b_ref, wb_ref, gq_ref, gk_ref, avg_ref, n_ref, q_ref, k_ref, v_ref, rq_ref, rk_ref, w_ref,
+     sem) = refs
+
+    @pl.when(pl.program_id(0) == 0)
+    def _():
+        laid.start(own_ref[0], block_refs, w_ref, sem)
+
     z, _ = row_stats(x_ref[...].astype(F32))
-    normed = (z * g_ref[...] + b_ref[...]).astype(BF16)
-    n_ref[...] = normed
+    n_ref[...] = (z * g_ref[...] + b_ref[...]).astype(BF16)
+
+    @pl.when(pl.program_id(0) == 0)
+    def _():
+        laid.wait(w_ref, sem)
+
+    normed = n_ref[...]
+    avg = avg_ref[...]
     width = q_ref.shape[1]
-    avg = avg_ref[...]
     for part in range(3):
         for col in range(0, width, 256):
-            at = part * width + col
-            pre = dot(normed, w_ref[:, at:at + 256]) + wb_ref[:, at:at + 256]
+            here = slice(col, col + 256)
+            cols = slice(part * width + col, part * width + col + 256)
+            pre = dot(normed, w_ref[:, cols]) + wb_ref[:, cols]
             if part == 2:
-                v_ref[:, col:col + 256] = pre.astype(BF16)
+                v_ref[:, here] = pre.astype(BF16)
                 continue
             high = pre.astype(BF16)
             low = (pre - high.astype(F32)).astype(BF16)
             center = pre - (dot(high, avg) + dot(low, avg))
             rstd = lax.rsqrt(dot((center * center).astype(BF16), avg) + NORM_EPS)
             gain = gk_ref if part else gq_ref
-            out = k_ref if part else q_ref
-            rout = rk_ref if part else rq_ref
-            out[:, col:col + 256] = (center * rstd * gain[:, col:col + 256]).astype(BF16)
-            rout[:, col:col + 256] = rstd.astype(BF16)
-
-
-def qkv_project(x, gain, bias, weight, wbias, gain_q, gain_k, avg):
+            (k_ref if part else q_ref)[:, here] = (center * rstd * gain[:, here]).astype(BF16)
+            (rk_ref if part else rq_ref)[:, here] = rstd.astype(BF16)
+
+
+def qkv_project(own, weight, x, gain, bias, wbias, gain_q, gain_k, avg):
+    blocks, laid = weight
     total, width = x.shape
     rows = 512
-    tile = pl.BlockSpec((rows, width), lambda i: (i, 0))
-    outs = [jax.ShapeDtypeStruct((total, width), BF16)] * 6
+    tile = pl.BlockSpec((rows, width), lambda i, *_: (i, 0))
+    vec = const_spec((1, width))
     return pl.pallas_call(
-        qkv_kernel,
-        grid=(total // rows,),
-        in_specs=[tile, const_spec((1, width)), const_spec((1, width)), const_spec(weight.shape),
-                  const_spec((1, 3 * width)), const_spec((1, width)), const_spec((1, width)),
-                  const_spec((256, 256))],
-        out_specs=[tile] * 6,
-        out_shape=outs,
+        functools.partial(qkv_kernel, count=len(blocks), laid=laid),
+        grid_spec=pltpu.PrefetchScalarGridSpec(
+            num_scalar_prefetch=1,
+            grid=(total // rows,),
+            in_specs=any_specs(len(blocks)) + [tile, vec, vec, const_spec((1, 3 * width)), vec, vec,
+                                               const_spec((256, 256))],
+            out_specs=[tile] * 6,
+            scratch_shapes=[pltpu.VMEM((width, 3 * width), BF16), pltpu.SemaphoreType.DMA(())]),
+        out_shape=[jax.ShapeDtypeStruct((total, width), BF16)] * 6,
         compiler_params=params(),
+        cost_estimate=cost(6 * total * width * width, total * width * 14),
         name="qkv_project",
-    )(x, gain, bias, weight, wbias, gain_q, gain_k, avg)
+    )(own, *blocks, x, gain, bias, wbias, gain_q, gain_k, avg)
 
 
 def half_masks(rows):
@@ -107,6 +154,7 @@
                 def _():
                     first = pl.multiple_of(jnp.minimum(aligned, total - blocks * BLK), 16)
                     body(slot, start, start + length, first, blocks)
+
         return carry
 
     lax.fori_loop(0, slots, one, 0)
@@ -127,9 +175,10 @@
     return (lane == slot) | (lane == CONST_LANE)
 
 
-def fwd_kernel(len_ref, off_ref, q_ref, k_ref, v_ref, aq_ref, ak_ref, o_ref, l_ref):
+def fwd_kernel(len_ref, off_ref, q_ref, k_ref, v_ref, aq_ref, ak_ref, o_ref, e_ref, l_ref):
     total = q_ref.shape[0]
     o_ref[...] = v_ref[...]
+    e_ref[...] = jnp.zeros_like(e_ref)
     l_ref[...] = jnp.zeros_like(l_ref)
     left = half_masks(BLK)
     one = jnp.ones((BLK, 128), BF16)
@@ -152,8 +201,11 @@
             mixed = dot(shares, vals)
             keep = inside_rows(at, start, stop, BLK, 128)
             inv = 1.0 / mixed[:, 128:]
-            o_ref[pl.ds(at, BLK), :] = jnp.where(
-                keep, mixed[:, :128] * inv, o_ref[pl.ds(at, BLK), :].astype(F32)).astype(BF16)
+            out = mixed[:, :128] * inv
+            high = out.astype(BF16)
+            rest = out - high.astype(F32)
+            o_ref[pl.ds(at, BLK), :] = jnp.where(keep, high, o_ref[pl.ds(at, BLK), :])
+            e_ref[pl.ds(at, BLK), :] = jnp.where(keep, rest.astype(BF16), e_ref[pl.ds(at, BLK), :])
             l_ref[pl.ds(at, BLK), :] = jnp.where(keep, inv, l_ref[pl.ds(at, BLK), :])
             return carry
 
@@ -171,9 +223,10 @@
             num_scalar_prefetch=2,
             grid=(width // 128,),
             in_specs=[pair, pair, pair, const_spec((total, 128)), const_spec((total, 128))],
-            out_specs=[pair, pair]),
-        out_shape=[jax.ShapeDtypeStruct((total, width), BF16), jax.ShapeDtypeStruct((total, width), F32)],
+            out_specs=[pair] * 3),
+        out_shape=[jax.ShapeDtypeStruct((total, width), BF16)] * 2 + [jax.ShapeDtypeStruct((total, width), F32)],
         compiler_params=params(),
+        cost_estimate=cost(5 * total * total * width, total * width * 14),
         name="attention_forward",
     )(lengths, offsets, q, k, v, code_q, code_k)
 
@@ -267,6 +320,7 @@
             scratch_shapes=[pltpu.VMEM((total, 128), F32)] * 3 + [pltpu.VMEM((128, MAX_BLOCKS * BLK), F32)] * 2),
         out_shape=[jax.ShapeDtypeStruct((total, width), BF16)] * 3 + [jax.ShapeDtypeStruct((1, width), F32)] * 2,
         compiler_params=params(),
+        cost_estimate=cost(8 * total * total * width, total * width * 20),
         name="attention_backward",
     )(lengths, offsets, q, k, v, grad, delta, rstd_q, rstd_k, code_q, code_k, gain_q, gain_k, avg)
 
@@ -281,20 +335,24 @@
     return jnp.where(up >= 0, 1.0 - tail, tail), density * 0.3989422804014327
 
 
-def mlp_kernel(perm_ref, x_ref, c_ref, m_ref, p_ref, l_ref, wo_ref, bo_ref, g2_ref, b2_ref, wu_ref, bu_ref, wd_ref,
-               bd_ref, sum_ref,
-               out_ref, gh_ref, do_ref, da_ref, dwo_ref, dwu_ref, dwd_ref, dbo_ref, dg2_ref, db2_ref, dbu_ref, dbd_ref,
-               awo, awu, awd):
+def mlp_kernel(*refs, count_w, laid):
+    block_refs, refs = refs[:count_w], refs[count_w:]
+    (x_ref, c_ref, m_ref, e_ref, l_ref, p_ref, bo_ref, g2_ref, b2_ref, bu_ref, bd_ref, sum_ref,
+     out_ref, gh_ref, do_ref, da_ref, dw_ref, dbo_ref, dg2_ref, db2_ref, dbu_ref, dbd_ref,
+     awo, awu, awd, wo_ref, wu_ref, wd_ref, sems) = refs
     step = pl.program_id(0)
-    parts = perm_ref.shape[0]
-    count = pl.num_programs(0) - parts
+    count = pl.num_programs(0) - PARTS
     width = x_ref.shape[1]
-    hidden_width = wu_ref.shape[1]
+    hidden_width = wd_ref.shape[0]
 
     @pl.when(step == 0)
     def _():
+        for i, (part, dst) in enumerate(zip(laid, (wo_ref, wu_ref, wd_ref))):
+            part.start(0, block_refs, dst, sems.at[i])
         for ref in (awo, awu, awd, dbo_ref, dg2_ref, db2_ref, dbu_ref, dbd_ref):
             ref[...] = jnp.zeros(ref.shape, ref.dtype)
+        for i, (part, dst) in enumerate(zip(laid, (wo_ref, wu_ref, wd_ref))):
+            part.wait(dst, sems.at[i])
 
     @pl.when(step < count)
     def _():
@@ -331,10 +389,9 @@
         dbo_ref[...] += jnp.sum(grad_hidden, axis=0, keepdims=True)
         awo[...] += dot(mixed, branch, TN)
         grad_mixed = dot(branch, wo_ref[...], NT)
-        inv = l_ref[...]
-        scaled = grad_mixed * inv
-        do_ref[...] = scaled.astype(BF16)
-        prod = scaled * mixed.astype(F32)
+        scaled = (grad_mixed * l_ref[...]).astype(BF16)
+        do_ref[...] = scaled
+        prod = scaled.astype(F32) * (mixed.astype(F32) + e_ref[...].astype(F32))
         high = prod.astype(BF16)
         low = (prod - high.astype(F32)).astype(BF16)
         lane = lax.broadcasted_iota(jnp.int32, (prod.shape[0], 256), 1) % HD
@@ -347,85 +404,112 @@
 
     @pl.when(step >= count)
     def _():
-        part = perm_ref[jnp.maximum(step - count, 0)]
-        for acc, ref in ((awo, dwo_ref), (awu, dwu_ref), (awd, dwd_ref)):
-            rows = ref.shape[0]
-            ref[...] = acc[pl.ds(pl.multiple_of(part * rows, 16), rows), :].astype(BF16)
-
-
-def mlp_both(perm, x, cot, mixed, pad, linv, wo, bo, g2, b2, wu, bu, wd, bd, summer):
+        part = jnp.maximum(step - count, 0)
+        short, tall = width // PARTS, hidden_width // PARTS
+        narrow = pl.ds(pl.multiple_of(part * short, 16), short)
+        dw_ref[:short, :] = awo[narrow, :].astype(BF16)
+        for i in range(hidden_width // width):
+            dw_ref[(i + 1) * short:(i + 2) * short, :] = awu[narrow, i * width:(i + 1) * width].astype(BF16)
+        dw_ref[dw_ref.shape[0] - tall:, :] = awd[pl.ds(pl.multiple_of(part * tall, 16), tall), :].astype(BF16)
+
+
+def mlp_both(weight, x, cot, mixed, rest, linv, pad, bo, g2, b2, bu, bd, summer):
+    blocks, laid = weight
     total, width = x.shape
-    ff = wu.shape[1]
-    parts = perm.shape[0]
+    ff = bu.shape[1]
     rows = 256
     count = total // rows
-    tile = pl.BlockSpec((rows, width), lambda i, *_: (jnp.minimum(i, count - 1), 0))
-
-    def grad_spec(shape):
-        return pl.BlockSpec((shape[0] // parts, shape[1]), lambda i, *_: (jnp.maximum(i - count, 0), 0))
-
-    vec = pl.BlockSpec((1, width), lambda i, *_: (0, 0))
-    vec_ff = pl.BlockSpec((1, ff), lambda i, *_: (0, 0))
+
+    def row_spec(cols):
+        return pl.BlockSpec((rows, cols), lambda i: (jnp.minimum(i, count - 1), 0))
+
+    shapes = ((width, width), (width, ff), (ff, width))
+    vectors = (width, width, width, ff, width)
+    tile = row_spec(width)
+    vec = const_spec((1, width))
+    each = (width + 2 * ff) // PARTS
     return pl.pallas_call(
-        mlp_kernel,
+        functools.partial(mlp_kernel, count_w=len(blocks), laid=laid),
+        grid=(count + PARTS,),
+        in_specs=any_specs(len(blocks)) + [tile] * 5 + [row_spec(1), vec, vec, vec, const_spec((1, ff)), vec,
+                                                        const_spec((256, 256))],
+        out_specs=[tile] * 4 + [pl.BlockSpec((each, width), lambda i: (jnp.maximum(i - count, 0), 0))]
+        + [pl.BlockSpec((1, n), lambda i: (0, 0)) for n in vectors],
+        scratch_shapes=[pltpu.VMEM(s, F32) for s in shapes] + [pltpu.VMEM(s, BF16) for s in shapes] + [
+            pltpu.SemaphoreType.DMA((3,))],
+        out_shape=[jax.ShapeDtypeStruct((total, width), BF16), jax.ShapeDtypeStruct((total, width), F32)]
+        + [jax.ShapeDtypeStruct((total, width), BF16)] * 2
+        + [jax.ShapeDtypeStruct((each * PARTS, width), BF16)]
+        + [jax.ShapeDtypeStruct((1, n), F32) for n in vectors],
+        compiler_params=params(),
+        cost_estimate=cost(2 * total * width * (3 * width + 6 * ff), total * width * 24),
+        name="mlp_both",
+    )(*blocks, x, cot, mixed, rest, linv, pad, bo, g2, b2, bu, bd, summer)
+
+
+def dqkv_kernel(perm_ref, n_ref, gq_ref, gk_ref, gv_ref, *refs, counts, sizes):
+    vectors, (send_ref, keep_ref, acc, boxes) = refs[:-4], refs[-4:]
+    total, width = n_ref.shape
+    rows = width // PARTS
+    half = PARTS // 2
+    each = 3 * rows + SMALL
+    ones = jnp.ones((8, total), BF16)
+    parts = (gq_ref, gk_ref, gv_ref)
+    for i, ref in enumerate(parts):
+        acc[:, i * width:(i + 1) * width] = dot(n_ref[...], ref[...], TN)
+    bias = jnp.concatenate([dot(ones, ref[...])[:1] for ref in parts], axis=1)
+    boxes[...] = jnp.zeros_like(boxes)
+    at = 0
+    for i, (count, size) in enumerate(zip(counts, sizes)):
+        whole = bias if count == 0 else vectors[at][...]
+        at += count
+        span = size * PARTS
+        fold = whole[:, :span]
+        for extra in range(span, whole.shape[1], span):
+            fold = fold + whole[:, extra:extra + span]
+        for a in range(PARTS):
+            boxes[a, i:i + 1, :size] = fold[:, a * size:(a + 1) * size]
+    for part in range(PARTS):
+        out = keep_ref if part >= half else send_ref
+        place = perm_ref[part]
+        at = (part % half) * each
+        for i in range(3):
+            out[at + i * rows:at + (i + 1) * rows, :] = acc[
+                pl.ds(pl.multiple_of(place * rows, 8), rows), i * width:(i + 1) * width].astype(BF16)
+        out[at + 3 * rows:at + each, :] = boxes[place].astype(BF16)
+
+
+def qkv_weight_grad(perm, normed, gq, gk, gv, vectors, sizes):
+    total, width = normed.shape
+    vmem = pl.BlockSpec(memory_space=pltpu.VMEM)
+    given = [v for v in vectors if v is not None]
+    each = 3 * width // PARTS + SMALL
+    return pl.pallas_call(
+        functools.partial(dqkv_kernel, counts=[int(v is not None) for v in vectors], sizes=sizes),
         grid_spec=pltpu.PrefetchScalarGridSpec(
             num_scalar_prefetch=1,
-            grid=(count + parts,),
-            in_specs=[tile, tile, tile, pl.BlockSpec((rows, 1), lambda i, *_: (jnp.minimum(i, count - 1), 0)), tile,
-                      const_spec(wo.shape), const_spec((1, width)), const_spec((1, width)), const_spec((1, width)),
-                      const_spec(wu.shape), const_spec((1, ff)), const_spec(wd.shape), const_spec((1, width)),
-                      const_spec((256, 256))],
-            out_specs=[tile, tile, tile, tile, grad_spec(wo.shape), grad_spec(wu.shape), grad_spec(wd.shape),
-                       vec, vec, vec, vec_ff, vec],
-            scratch_shapes=[pltpu.VMEM(wo.shape, F32), pltpu.VMEM(wu.shape, F32), pltpu.VMEM(wd.shape, F32)]),
-        out_shape=[jax.ShapeDtypeStruct((total, width), BF16), jax.ShapeDtypeStruct((total, width), F32),
-                   jax.ShapeDtypeStruct((total, width), BF16), jax.ShapeDtypeStruct((total, width), BF16),
-                   jax.ShapeDtypeStruct(wo.shape, BF16), jax.ShapeDtypeStruct(wu.shape, BF16),
-                   jax.ShapeDtypeStruct(wd.shape, BF16)]
-        + [jax.ShapeDtypeStruct((1, n), F32) for n in (width, width, width, ff, width)],
+            grid=(),
+            in_specs=[vmem] * (4 + len(given)),
+            out_specs=[vmem] * 2,
+            scratch_shapes=[pltpu.VMEM((width, 3 * width), F32), pltpu.VMEM((PARTS, SMALL, width), F32)]),
+        out_shape=[jax.ShapeDtypeStruct((each * PARTS // 2, width), BF16)] * 2,
         compiler_params=params(),
-        name="mlp_both",
-    )(perm, x, cot, mixed, pad, linv, wo, bo, g2, b2, wu, bu, wd, bd, summer)
-
-
-def dqkv_kernel(perm_ref, n_ref, gq_ref, gk_ref, gv_ref, dw_ref, db_ref, acc):
-    parts = perm_ref.shape[0]
-    total, width = n_ref.shape
-    rows = width // parts
-    ones = jnp.ones((8, total), BF16)
-    for i, ref in enumerate((gq_ref, gk_ref, gv_ref)):
-        @pl.when(pl.program_id(0) == i)
-        def _():
-            acc[...] = dot(n_ref[...], ref[...], TN)
-            db_ref[...] = dot(ones, ref[...])[:1]
-    for part in range(parts):
-        dw_ref[part * rows:(part + 1) * rows, :] = acc[
-            pl.ds(pl.multiple_of(perm_ref[part] * rows, 8), rows), :].astype(BF16)
-
-
-def qkv_weight_grad(perm, normed, gq, gk, gv):
-    total, width = normed.shape
-    return pl.pallas_call(
-        dqkv_kernel,
-        grid_spec=pltpu.PrefetchScalarGridSpec(
-            num_scalar_prefetch=1,
-            grid=(3,),
-            in_specs=[const_spec((total, width))] * 4,
-            out_specs=[pl.BlockSpec((width, width), lambda i, *_: (0, i)), pl.BlockSpec((1, width), lambda i, *_: (0, i))],
-            scratch_shapes=[pltpu.VMEM((width, width), F32)]),
-        out_shape=[jax.ShapeDtypeStruct((width, 3 * width), BF16), jax.ShapeDtypeStruct((1, 3 * width), F32)],
-        compiler_params=params(),
+        cost_estimate=cost(6 * total * width * width, total * width * 8),
         name="qkv_weight_grad",
-    )(perm, normed, gq, gk, gv)
-
-
-def dinput_kernel(x_ref, gh_ref, gq_ref, gk_ref, gv_ref, w_ref, g_ref, out_ref, dg_ref, db_ref):
+    )(perm, normed, gq, gk, gv, *given)
+
+
+def dinput_kernel(own_ref, *refs, count, laid):
+    block_refs, refs = refs[:count], refs[count:]
+    gq_ref, gk_ref, gv_ref, x_ref, gh_ref, g_ref, out_ref, dg_ref, db_ref, w_ref, sem = refs
     width = x_ref.shape[1]
 
     @pl.when(pl.program_id(0) == 0)
     def _():
+        laid.start(own_ref[0], block_refs, w_ref, sem)
         dg_ref[...] = jnp.zeros_like(dg_ref)
         db_ref[...] = jnp.zeros_like(db_ref)
+        laid.wait(w_ref, sem)
 
     grad = dot(gq_ref[...], w_ref[:, :width], NT)
     grad += dot(gk_ref[...], w_ref[:, width:2 * width], NT)
@@ -438,56 +522,198 @@
                                          - z * jnp.mean(inner * z, axis=-1, keepdims=True))
 
 
-def input_grad(x, gh, gq, gk, gv, weight, gain):
+def input_grad(own, weight, gq, gk, gv, x, gh, gain):
+    blocks, laid = weight
     total, width = x.shape
     rows = 512
-    tile = pl.BlockSpec((rows, width), lambda i: (i, 0))
-    vec = pl.BlockSpec((1, width), lambda i: (0, 0))
+    tile = pl.BlockSpec((rows, width), lambda i, *_: (i, 0))
+    vec = pl.BlockSpec((1, width), lambda i, *_: (0, 0))
     return pl.pallas_call(
-        dinput_kernel,
-        grid=(total // rows,),
-        in_specs=[tile] * 5 + [const_spec(weight.shape), const_spec((1, width))],
-        out_specs=[tile, vec, vec],
+        functools.partial(dinput_kernel, count=len(blocks), laid=laid),
+        grid_spec=pltpu.PrefetchScalarGridSpec(
+            num_scalar_prefetch=1,
+            grid=(total // rows,),
+            in_specs=any_specs(len(blocks)) + [tile] * 5 + [const_spec((1, width))],
+            out_specs=[tile, vec, vec],
+            scratch_shapes=[pltpu.VMEM((width, 3 * width), BF16), pltpu.SemaphoreType.DMA(())]),
         out_shape=[jax.ShapeDtypeStruct((total, width), F32)] + [jax.ShapeDtypeStruct((1, width), F32)] * 2,
         compiler_params=params(),
+        cost_estimate=cost(6 * total * width * width, total * width * 16),
         name="input_grad",
-    )(x, gh, gq, gk, gv, weight, gain)
-
-
-def gather(block):
-    return lax.all_gather(block, "shard", axis=0, tiled=True)
-
-
-def reduce_owned(grad):
-    own = lax.psum_scatter(grad, "shard", scatter_dimension=0, tiled=True)
-    return lax.psum(own, "rep").astype(F32)
-
-
-PARTS = 8
-
-
-def block_order():
-    return jnp.arange(PARTS, dtype=jnp.int32)
+    )(own, *blocks, gq, gk, gv, x, gh, gain)
+
+
+def pack_kernel(w_ref, *refs):
+    out = refs[-1]
+    rows = w_ref.shape[0]
+    width = out.shape[1]
+    for i in range(3):
+        out[i * rows:(i + 1) * rows, :] = w_ref[:, i * width:(i + 1) * width]
+    box = jnp.zeros((1, width), F32)
+    out[3 * rows:, :] = jnp.zeros((SMALL, width), BF16)
+    for i, ref in enumerate(refs[:-1]):
+        out[3 * rows + i:3 * rows + i + 1, :ref.shape[1]] = ref[...]
+
+
+def pack_share(weight, vectors):
+    rows, width = weight.shape[0], weight.shape[1] // 3
+    return pl.pallas_call(
+        pack_kernel, out_shape=jax.ShapeDtypeStruct((3 * rows + SMALL, width), BF16), name="pack_share",
+    )(weight, *[v[None] for v in vectors])
+
+
+def unpack_kernel(own_ref, *refs, sizes, codes):
+    blocks, outs, box = refs[:len(codes)], refs[len(codes):-1], refs[-1]
+    for code, ref in zip(codes, blocks):
+        box[own_ref[0] ^ code] = ref[...].astype(F32)
+    for a in range(PARTS):
+        block = box[a]
+        for i, (size, out) in enumerate(zip(sizes, outs)):
+            out[:, a * size:(a + 1) * size] = block[i:i + 1, :size]
+
+
+def unpack_small(own, blocks, places, sizes):
+    width = blocks[0].shape[1]
+
+    def spec(row):
+        return pl.BlockSpec((SMALL, width), lambda i, *_: (row // SMALL, 0))
+
+    return pl.pallas_call(
+        functools.partial(unpack_kernel, sizes=sizes, codes=[c for _, _, c in places]),
+        grid_spec=pltpu.PrefetchScalarGridSpec(
+            num_scalar_prefetch=1, grid=(1,), in_specs=[spec(row) for _, row, _ in places],
+            out_specs=[pl.BlockSpec((1, PARTS * n), lambda i, *_: (0, 0)) for n in sizes],
+            scratch_shapes=[pltpu.VMEM((PARTS, SMALL, width), F32)]),
+        out_shape=[jax.ShapeDtypeStruct((1, PARTS * n), F32) for n in sizes],
+        name="unpack_small",
+    )(own, *[blocks[which] for which, _, _ in places])
+
+
+def swap(value, code):
+    return lax.ppermute(value, "shard", [(i, i ^ code) for i in range(8)])
+
+
+def swap_mixed(value, even, odd):
+    return lax.ppermute(value, "shard", [(i, i ^ (odd if i % 2 else even)) for i in range(8)])
+
+
+def along(value, pairs):
+    return lax.ppermute(value, "rep", pairs)
+
+
+def total_of(*values):
+    out = values[0].astype(F32)
+    for value in values[1:]:
+        out = out + value.astype(F32)
+    return out
+
+
+class Chips:
+    def __init__(self):
+        self.own = lax.axis_index("shard").astype(jnp.int32)
+        self.rep = lax.axis_index("rep")
+        odd = self.own % 2 == 1
+        first = jnp.array([1, 3, 5, 7, 0, 4, 2, 6], jnp.int32)
+        second = jnp.array([1, 5, 3, 7, 0, 2, 4, 6], jnp.int32)
+        self.perm = jnp.where(odd, second, first) ^ self.own
+
+    def gather_share(self, weight, vectors, sizes):
+        share = pack_share(weight, vectors)
+        each = share.shape[0]
+        rows = weight.shape[0]
+        right, up, far = swap(share, 2), swap(share, 4), swap(share, 6)
+        self.fence = far
+        others = swap(jnp.concatenate([share, right, up, far], axis=0), 1)
+        blocks = [share, right, up, far, others]
+        starts = [(0, 0, 0), (1, 0, 2), (2, 0, 4), (3, 0, 6)] + [(4, i * each, c) for i, c in enumerate((1, 3, 5, 7))]
+        laid = Laid([(w, r + i * rows, rows, c, i) for w, r, c in starts for i in range(3)], True)
+        small = unpack_small(self.own[None], blocks, [(w, r + 3 * rows, c) for w, r, c in starts], sizes)
+        return (blocks, laid), small
+
+    def gather_rest(self, wo, wu, wd):
+        rows, width = wo.shape
+        tall = wd.shape[0]
+        cuts = wu.shape[1] // width
+        share = jnp.concatenate([wo] + [wu[:, i * width:(i + 1) * width] for i in range(cuts)] + [wd], axis=0)
+        each = share.shape[0]
+        share, _ = lax.optimization_barrier((share, self.fence))
+        whole = lax.all_gather(share, "shard", axis=0, tiled=True)
+        laid_o = Laid([(0, a * each, rows, a, 0) for a in range(PARTS)], False)
+        laid_u = Laid([(0, a * each + (i + 1) * rows, rows, a, i) for a in range(PARTS) for i in range(cuts)], False)
+        laid_d = Laid([(0, (a + 1) * each - tall, tall, a, 0) for a in range(PARTS)], False)
+        return [whole], (laid_o, laid_u, laid_d)
+
+    def reduce_rest(self, stacked, width, ff):
+        own = lax.psum_scatter(stacked, "shard", scatter_dimension=0, tiled=True)
+        own = lax.psum(own, "rep")
+        rows, cuts, tall = width // PARTS, ff // width, ff // PARTS
+        own = own.astype(F32)
+        up = jnp.concatenate([own[(i + 1) * rows:(i + 2) * rows] for i in range(cuts)], axis=1)
+        return own[:rows], up, own[own.shape[0] - tall:]
+
+    def reduce_share(self, send, keep, sizes):
+        rows = keep.shape[0] // 4
+        got = swap(send, 1)
+        tail = total_of(keep[2 * rows:], got[2 * rows:]).astype(BF16)
+        more = swap_mixed(tail, 2, 4)
+        near = total_of(keep[rows:2 * rows], got[rows:2 * rows], more[rows:]).astype(BF16)
+        last = swap_mixed(near, 4, 2)
+        mine = total_of(keep[:rows], got[:rows], more[:rows], last).astype(BF16)
+        inner = total_of(mine, along(mine, [(0, 1), (3, 2)])).astype(BF16)
+        whole = total_of(inner, along(inner, [(1, 2), (2, 1)])).astype(BF16)
+        outer = along(whole, [(1, 0), (2, 3)])
+        own = jnp.where((self.rep == 0) | (self.rep == 3), outer, whole).astype(F32)
+        cut = (rows - SMALL) // 3
+        weight = jnp.concatenate([own[i * cut:(i + 1) * cut] for i in range(3)], axis=1)
+        return weight, [own[3 * cut + i, :n] for i, n in enumerate(sizes)]
+
+
+class Anywhere:
+    def __init__(self, shards):
+        self.shards = shards
+        self.own = jnp.zeros((), jnp.int32)
+        self.perm = jnp.arange(PARTS, dtype=jnp.int32)
+
+    def gather(self, value):
+        return lax.all_gather(value, "shard", axis=0, tiled=True)
+
+    def gather_share(self, weight, vectors, sizes):
+        small = [self.gather(v).astype(F32)[None] for v in vectors]
+        return ([self.gather(weight)], Laid([(0, 0, None, 0, 0)], True)), small
+
+    def gather_rest(self, wo, wu, wd):
+        return [self.gather(w) for w in (wo, wu, wd)], tuple(Laid([(i, 0, None, 0, 0)], False) for i in range(3))
+
+    def reduce(self, grad):
+        return lax.psum(lax.psum_scatter(grad, "shard", scatter_dimension=0, tiled=True), "rep").astype(F32)
+
+    def reduce_rest(self, stacked, width, ff):
+        rows, cuts, tall = width // PARTS, ff // width, ff // PARTS
+        each = stacked.reshape(PARTS, -1, width)
+        up = jnp.concatenate([each[:, (i + 1) * rows:(i + 2) * rows].reshape(width, width) for i in range(cuts)], axis=1)
+        out = each[:, :rows].reshape(width, width)
+        return self.reduce(out), self.reduce(up), self.reduce(each[:, each.shape[1] - tall:].reshape(ff, width))
+
+    def reduce_share(self, send, keep, sizes):
+        width = send.shape[1]
+        each = jnp.concatenate([send, keep], axis=0).reshape(PARTS, -1, width)
+        cut = (each.shape[1] - SMALL) // 3
+        weight = jnp.concatenate([each[:, i * cut:(i + 1) * cut].reshape(width, width) for i in range(3)], axis=1)
+        small = [self.reduce(each[:, 3 * cut + i, :n * self.shards // PARTS].reshape(-1)) for i, n in enumerate(sizes)]
+        return self.reduce(weight), small
 
 
 def on_device(shards, reps, inputs, cotangent, picture_ids, picture_lengths, picture_offsets, padding, ln1_gain,
               ln1_bias, qkv_weight, qkv_bias, query_gain, key_gain, out_weight, out_bias, ln2_gain, ln2_bias,
               up_weight, up_bias, down_weight, down_bias):
-    total, width = inputs.shape
-    pairs = width // 128
+    _, width = inputs.shape
+    chips = Chips() if (shards, reps) == (PARTS, 4) else Anywhere(shards)
+    own = chips.own[None]
     small = (ln1_gain, ln1_bias, qkv_bias, query_gain, key_gain, out_bias, ln2_gain, ln2_bias, up_bias, down_bias)
-    sizes = [a.shape[0] for a in small]
-    packed = gather(jnp.concatenate(small)[None])
-    at = 0
-    full = []
-    for size in sizes:
-        full.append(packed[:, at:at + size].reshape(1, shards * size).astype(F32))
-        at += size
+    sizes = tuple(a.shape[0] for a in small)
+    weight_qkv, full = chips.gather_share(qkv_weight, small, sizes)
+    weight_rest = chips.gather_rest(out_weight, up_weight, down_weight)
     gain_one, shift_one, bias_qkv, gain_query, gain_key, bias_out, gain_two, shift_two, bias_up, bias_down = full
-    weight_qkv = gather(qkv_weight)
-    weight_out = gather(out_weight)
-    weight_up = gather(up_weight)
-    weight_down = gather(down_weight)
 
     lengths = picture_lengths.reshape(-1)
     offsets = picture_offsets.reshape(-1)
@@ -504,31 +730,19 @@
     gain_k = jnp.tile(gain_key, (1, HEADS))
 
     normed, q, k, v, rstd_q, rstd_k = qkv_project(
-        inputs, gain_one, shift_one, weight_qkv, bias_qkv, gain_q * (HD ** -0.5 * LOG2E), gain_k, avg)
-    mixed, linv = attention_forward(lengths, offsets, q, k, v, code_q, code_k)
-    perm = block_order()
-    (output, grad_hidden, grad_scaled, delta, dwo, dwu, dwd, dbo, dg2, db2, dbu, dbd) = mlp_both(
-        perm, inputs, cotangent, mixed, padding.astype(F32)[:, None], linv, weight_out, bias_out, gain_two, shift_two,
-        weight_up, bias_up, weight_down, bias_down, summer)
-    own_down = reduce_owned(dwd)
-    own_up = reduce_owned(dwu)
-    own_out = reduce_owned(dwo)
+        own, weight_qkv, inputs, gain_one, shift_one, bias_qkv, gain_q * (HD ** -0.5 * LOG2E), gain_k, avg)
+    mixed, mixed_rest, linv = attention_forward(lengths, offsets, q, k, v, code_q, code_k)
+    output, grad_hidden, scaled, delta, stacked, dbo, dg2, db2, dbu, dbd = mlp_both(
+        weight_rest, inputs, cotangent, mixed, mixed_rest, linv, padding.astype(F32)[:, None], bias_out, gain_two,
+        shift_two, bias_up, bias_down, summer)
+    own_out, own_up, own_down = chips.reduce_rest(stacked, width, bias_up.shape[1])
     gq, gk, gv, dgq, dgk = attention_backward(
-        lengths, offsets, q, k, v, grad_scaled, delta, rstd_q, rstd_k, code_q, code_k, gain_q, gain_k,
-        avg[:128, :128])
-    dw, db = qkv_weight_grad(perm, normed, gq, gk, gv)
-    own_qkv = reduce_owned(dw)
-    grad_input, dg1, db1 = input_grad(inputs, grad_hidden, gq, gk, gv, weight_qkv, gain_one)
-    dgq = jnp.sum(dgq.reshape(HEADS, HD), axis=0)
-    dgk = jnp.sum(dgk.reshape(HEADS, HD), axis=0)
-    vectors = (dg1, db1, db, dgq, dgk, dbo, dg2, db2, dbu, dbd)
-    rows = jnp.concatenate([g.reshape(shards, -1) for g in vectors], axis=1)
-    own = reduce_owned(rows)[0]
-    at = 0
-    owned = []
-    for size in sizes:
-        owned.append(own[at:at + size])
-        at += size
+        lengths, offsets, q, k, v, scaled, delta, rstd_q, rstd_k, code_q, code_k, gain_q, gain_k, avg[:128, :128])
+    grad_input, dg1, db1 = input_grad(own, weight_qkv, gq, gk, gv, inputs, grad_hidden, gain_one)
+    send, keep = qkv_weight_grad(
+        chips.perm, normed, gq, gk, gv, (dg1, db1, None, dgq, dgk, dbo, dg2, db2, dbu, dbd),
+        tuple(n * shards // PARTS for n in sizes))
+    own_qkv, owned = chips.reduce_share(send, keep, sizes)
     og1, ob1, obqkv, ogq, ogk, obo, og2, ob2, obu, obd = owned
     return (output, grad_input, og1, ob1, own_qkv, obqkv, ogq, ogk, own_out, obo, og2, ob2, own_up, obu, own_down, obd)
 

time: 636 us -> 507 us (0.80)
  waiting for transfers between devices: 235 us -> 137 us
  blocking collectives: 63.5 us -> 0 us
  starting transfers between devices: 0.35 us -> 38.7 us
  Pallas kernels: 274 us -> 281 us
    reduce_scatter x4 -> x1, waiting for transfers between devices: 184 us -> 0.02 us  [reduce_rest(): own = lax.psum_scatter(stacked, 'shard', scatter_dimension=0, tiled=True)]
    ppermute x0 -> x10, waiting for transfers between devices: none -> 94 us  [the longest x3 49.7 us: along(): return lax.ppermute(value, 'rep', pairs)]
    unnamed x2 -> x0, blocking collectives: 50.9 us -> none
    ppermute x0 -> x10, starting transfers between devices: none -> 38.6 us  [the longest x2 21.6 us: swap_mixed(): lax.ppermute(value, 'shard', [(i, i ^ (odd if i % 2 else even)) for i in...]
    all_gather x4 -> x1, waiting for transfers between devices: 28.1 us -> 0.01 us  [gather_rest(): whole = lax.all_gather(share, 'shard', axis=0, tiled=True)]
    psum x1, waiting for transfers between devices: 18.3 us -> 43.1 us  [reduce_rest(): own = lax.psum(own, 'rep')]
    psum x1 -> x0, blocking collectives: 12.6 us -> none  [reduce_owned(): return lax.psum(own, 'rep').astype(F32)]
    concatenate x2 -> x1, local copies, waits for them, and re-layouts: 6.9 us -> 0.04 us  [gather_rest(): jnp.concatenate([wo] + [wu[:, i * width:(i + 1) * width] for i in range(c...]
  transfers between devices with their start and end apart: 9 -> 13, of which waited for: 5 -> 9; matrix products, arithmetic and copies ran while one was open for 5% -> 4% of each run, Pallas kernels for 27% -> 35%
where the time goes in v2:
time: 507 us; the launch traced here: 500 us
  Pallas kernels  281 us (55%)
  waiting for transfers between devices  137 us (27%)
  starting transfers between devices  38.7 us (8%)
  local copies, waits for them, and re-layouts  17.6 us (3%)
  between operations  14.3 us (3%)
  other arithmetic  10.7 us (2%)
    pallas_call x1, Pallas kernels, mlp_both(): pl.pallas_call(functools.partial(mlp_kernel, count_w=len(blocks), laid=la...  103 us
    pallas_call x1, Pallas kernels, attention_backward(): pl.pallas_call(bwd_kernel, grid_spec=pltpu.PrefetchScalarGridSpec(num_sca...  71 us
    pallas_call x1, Pallas kernels, attention_forward(): pl.pallas_call(fwd_kernel, grid_spec=pltpu.PrefetchScalarGridSpec(num_sca...  50.1 us
    ppermute x3, waiting for transfers between devices, along(): return lax.ppermute(value, 'rep', pairs)  49.7 us
    psum x1, waiting for transfers between devices, reduce_rest(): own = lax.psum(own, 'rep')  43.1 us
    ppermute x5, waiting for transfers between devices, swap(): return lax.ppermute(value, 'shard', [(i, i ^ code) for i in range(8)])  24.3 us
    ppermute x2, starting transfers between devices, swap_mixed(): lax.ppermute(value, 'shard', [(i, i ^ (odd if i % 2 else even)) for i in...  21.6 us
    ppermute x2, waiting for transfers between devices, swap_mixed(): lax.ppermute(value, 'shard', [(i, i ^ (odd if i % 2 else even)) for i in...  20.1 us
  transfers between devices with their start and end apart: 13, of which 9 were waited for; matrix products, arithmetic and copies ran while one was open for 4% of the time, Pallas kernels for 35%

profile of v2, /device:TPU:0, one launch (start us, length us, event | category | flops | bytes accessed | tf_op | source)
XLA Modules:
  0.0 499.5 jit_solution(6714001688434282198)
XLA Ops:
  7.2 0.0 all-gather.2.cloned.1.call-start
  7.2 1.3 broadcast_in_dim.44.refs_2_
  8.5 1.2 broadcast_in_dim.50.refs_8_
  9.8 1.9 pack_share.1.refs_0_
  11.7 3.9 collective-permute-start
  15.6 0.9 constant_dynamic-update-slice_fusion.1
  16.6 1.0 slice_dynamic-update-slice_fusion.3
  17.6 0.9 slice_dynamic-update-slice_fusion.2
  18.6 7.9 %collective-permute-done.refs_3_ = bf16[304,768]{1,0:T(8,128)(2,1)S(1)} collective-permute-done((bf16[304,768]{1,0:T(8,128)(2,1)}, bf16[304,768]{1,0:T(8,128)(2,1)S(1)}, u32[]{:S(2)}, u32[]{:S(2)}) %collective-permute-start) | collective-permute-done | bytes 466976 | tf_op jit(solution)/shard_map/ppermute | solution.py:593
  26.6 0.0 reduce-scatter.2.cloned.1.call-start
  26.7 1.8 collective-permute-start.2
  28.4 1.5 collective-permute-start.1
  29.9 8.7 %collective-permute-done.2.refs_2_ = bf16[304,768]{1,0:T(8,128)(2,1)S(1)} collective-permute-done((bf16[304,768]{1,0:T(8,128)(2,1)S(1)}, bf16[304,768]{1,0:T(8,128)(2,1)S(1)}, u32[]{:S(2)}, u32[]{:S(2)}) %collective-permute-start.2) | collective-permute-done | bytes 466976 | tf_op jit(solution)/shard_map/ppermute | solution.py:593
  38.6 4.0 collective-permute-done.1.refs_1_
  42.6 1.4 pad_maximum_fusion
  44.0 0.1 collective-permute-start.3
  44.1 1.3 copy.38.refs_6_
  45.4 0.8 multiply_convert_fusion.refs_11_
  46.2 0.8 compare_convert_fusion.refs_12_
  47.0 2.4 fusion.2
  49.4 1.3 copy-done
  50.6 1.6 unpack_small.1
  52.3 0.7 tile.23
  52.9 0.1 tile.24.gq_ref
  53.0 0.7 tile.26
  53.7 0.7 tile.27.refs_10_.gk_ref
  54.3 0.6 broadcast_multiply_fusion.refs_9_
  54.9 19.5 %qkv_project.1 = (bf16[2048,768]{1,0:T(8,128)(2,1)}, bf16[2048,768]{1,0:T(8,128)(2,1)}, bf16[2048,768]{1,0:T(8,128)(2,1)}, bf16[2048,768]{1,0:T(8,128)(2,1)}, bf...) custom-call(s32[1]{0:T(128)} %bitcast.10.own_ref, bf16[304,768]{1,0:T(8,128)(2,1)} %pack_share.1.refs_0_, ...), custom_call_target="tpu_custom_call" | custom-call | flops 7247757312 | bytes 22020096 | tf_op jit(solution)/shard_map/qkv_project/pallas_call | solution.py:120
  74.4 50.1 %attention_forward.1 = (bf16[2048,768]{1,0:T(8,128)(2,1)}, bf16[2048,768]{1,0:T(8,128)(2,1)}, f32[2048,768]{1,0:T(8,128)}) custom-call(s32[20]{0:T(128)} %bitcast.41, s32[20]{0:T(128)} %bitcast.43, bf16[2048,768]{1,0:T(8,128)(2,1)} %get-tuple-element.62.q_ref, bf16[2048,768]{1,0:T(8,128)(2,1)} %get-tuple-element.63.k_ref, ...), custom_call_target="tpu_custom_call" | custom-call | flops 16106127360 | bytes 22020096 | tf_op jit(solution)/shard_map/attention_forward/pallas_call | solution.py:220
  124.6 103.3 %mlp_both.1 = (bf16[2048,768]{1,0:T(8,128)(2,1)}, f32[2048,768]{1,0:T(8,128)}, bf16[2048,768]{1,0:T(8,128)(2,1)}, bf16[2048,768]{1,0:T(8,128)(2,1)}, bf16[6912,7...) custom-call(bf16[6912,768]{1,0:T(8,128)(2,1)} %all-gather.2.cloned.1, ...), custom_call_target="tpu_custom_call" | custom-call | flops 65229815808 | bytes 37748736 | tf_op jit(solution)/shard_map/mlp_both/pallas_call | solution.py:431
  228.0 0.0 all-reduce.2.cloned.1.call-start
  228.0 1.4 slice.128.avg_ref
  229.4 0.5 fusion.4.perm_ref
  229.9 71.0 %attention_backward.1 = (bf16[2048,768]{1,0:T(8,128)(2,1)}, bf16[2048,768]{1,0:T(8,128)(2,1)}, bf16[2048,768]{1,0:T(8,128)(2,1)}, f32[1,768]{1,0:T(1,128)}, f32[1,768]{1,0:T(1,128)}) custom-call(s32[20]{0:T(128)} %bitcast.42, s32[20]{0:T(128)} %bitcast.44, bf16[2048,768]{1,0:T(8,128)(2,1)} %get-tuple-element.62.q_ref, ...), custom_call_target="tpu_custom_call" | custom-call | flops 25769803776 | bytes 31457280 | tf_op jit(solution)/shard_map/attention_backward/pallas_call | solution.py:313
  300.9 17.2 %input_grad.1 = (f32[2048,768]{1,0:T(8,128)}, f32[1,768]{1,0:T(1,128)}, f32[1,768]{1,0:T(1,128)}) custom-call(s32[1]{0:T(128)} %bitcast.10.own_ref, bf16[304,768]{1,0:T(8,128)(2,1)} %pack_share.1.refs_0_, bf16[304,768]{1,0:T(8,128)(2,1)} %copy-done.5, bf16[304,768]{1,0:T(8,128)(2,1)} %copy-done.4, bf16[304,768]{1,0:T(8,128)(2,1)} %copy-done.3, ...), custom_call_target="tpu_custom_call" | custom-call | flops 7247757312 | bytes 25165824 | tf_op jit(solution)/shard_map/input_grad/pallas_call | solution.py:531
  318.2 16.2 %qkv_weight_grad.1 = (bf16[1216,768]{1,0:T(8,128)(2,1)}, bf16[1216,768]{1,0:T(8,128)(2,1)}) custom-call(s32[8]{0:T(128)} %fusion.4.perm_ref, bf16[2048,768]{1,0:T(8,128)(2,1)} %get-tuple-element.83.n_ref, bf16[2048,768]{1,0:T(8,128)(2,1)} %get-tuple-element.78.refs_5_.gq_ref, bf16[2048,768]{1,0:T(8,128)(2,1)} %get-tuple-element.79.refs_6_.gk_ref, ...), custom_call_target="tpu_custom_call" | custom-call | flops 7247757312 | bytes 12582912 | tf_op jit(solution)/shard_map/qkv_weight_grad/pallas_call | solution.py:487
  334.4 6.4 %collective-permute-start.4 = (bf16[1216,768]{1,0:T(8,128)(2,1)}, bf16[1216,768]{1,0:T(8,128)(2,1)S(1)}, u32[]{:S(2)}, u32[]{:S(2)}) collective-permute-start(bf16[1216,768]{1,0:T(8,128)(2,1)} %get-tuple-element.94), channel_id=1, source_target_pairs={{0,1},{1,0},{2,3},{3,2},{4,5},{5,4},{6,7},{7,6},{8,9},{9,8},{10,11... | collective-permute-start | bytes 5603336 | tf_op jit(solution)/shard_map/ppermute | solution.py:593
  340.8 3.7 collective-permute-done.4
  344.4 1.4 add_convert_fusion
  345.9 0.1 collective-permute-start.5
  345.9 13.6 %collective-permute-done.5 = bf16[608,768]{1,0:T(8,128)(2,1)S(1)} collective-permute-done((bf16[608,768]{1,0:T(8,128)(2,1)S(1)}, bf16[608,768]{1,0:T(8,128)(2,1)S(1)}, u32[]{:S(2)}, u32[]{:S(2)}) %collective-permute-start.5) | collective-permute-done | bytes 933920 | tf_op jit(solution)/shard_map/ppermute | solution.py:597
  359.5 0.2 add_convert_fusion.4
  359.7 21.6 %collective-permute-start.6 = (bf16[304,768]{1,0:T(8,128)(2,1)S(1)}, bf16[304,768]{1,0:T(8,128)(2,1)S(1)}, u32[]{:S(2)}, u32[]{:S(2)}) collective-permute-start(bf16[304,768]{1,0:T(8,128)(2,1)S(1)} %add_convert_fusion.4), channel_id=1, source_target_pairs={{0,4},{1,3},{2,6},{3,1},{4,0},{5,7},{6,2},{7,5},{8,12},{9,11},{10,... | collective-permute-start | bytes 1400840 | tf_op jit(solution)/shard_map/ppermute | solution.py:597
  381.3 6.5 %collective-permute-done.6 = bf16[304,768]{1,0:T(8,128)(2,1)S(1)} collective-permute-done((bf16[304,768]{1,0:T(8,128)(2,1)S(1)}, bf16[304,768]{1,0:T(8,128)(2,1)S(1)}, u32[]{:S(2)}, u32[]{:S(2)}) %collective-permute-start.6) | collective-permute-done | bytes 466976 | tf_op jit(solution)/shard_map/ppermute | solution.py:597
  387.8 0.2 add_convert_fusion.3
  388.1 1.3 collective-permute-start.7
  389.4 8.8 %collective-permute-done.7 = bf16[304,768]{1,0:T(8,128)(2,1)S(1)} collective-permute-done((bf16[304,768]{1,0:T(8,128)(2,1)S(1)}, bf16[304,768]{1,0:T(8,128)(2,1)S(1)}, u32[]{:S(2)}, u32[]{:S(2)}) %collective-permute-start.7) | collective-permute-done | bytes 466976 | tf_op jit(solution)/shard_map/ppermute | solution.py:601
  398.2 0.1 add_convert_fusion.2
  398.3 0.7 collective-permute-start.8
  399.0 0.1 add_convert_fusion.1
  399.1 1.3 collective-permute-start.9
  400.5 40.9 %collective-permute-done.9 = bf16[304,768]{1,0:T(8,128)(2,1)S(1)} collective-permute-done((bf16[304,768]{1,0:T(8,128)(2,1)S(1)}, bf16[304,768]{1,0:T(8,128)(2,1)S(1)}, u32[]{:S(2)}, u32[]{:S(2)}) %collective-permute-start.9) | collective-permute-done | bytes 466976 | tf_op jit(solution)/shard_map/ppermute | solution.py:601
  441.4 0.1 select_convert_fusion
  441.5 0.6 slice_reduce_fusion
  442.1 0.6 slice_reduce_fusion.1
  442.7 0.5 slice_bitcast_fusion.4
  443.2 0.5 slice_bitcast_fusion
  443.7 0.1 fusion.6
  443.8 1.0 pad_maximum_fusion.2
  444.8 43.1 %all-reduce.2.cloned.1.call-done = bf16[864,768]{1,0:T(8,128)(2,1)} async-done(((bf16[864,768]{1,0:T(8,128)(2,1)}), bf16[864,768]{1,0:T(8,128)(2,1)}) %all-reduce.2.cloned.1.call-update) | async-done | bytes 1327120 | tf_op jit(solution)/shard_map/psum | solution.py:648
  487.9 2.0 fusion.5
  489.9 1.1 pad_maximum_fusion.1
  491.0 0.6 copy-done.1
  491.7 1.1 slice.151
  (42 shorter events, 0.2 us)
Async XLA Ops:
  7.2 11.3 %copy-start.8 = (bf16[96,3072]{1,0:T(8,128)(2,1)S(1)}, bf16[96,3072]{1,0:T(8,128)(2,1)}, u32[]{:S(2)}) copy-start(bf16[96,3072]{1,0:T(8,128)(2,1)} %param.38) | copy-start | bytes 1769476
  7.2 117.4 %all-gather.2.cloned.1.call-start = ((), (), s32[]{:S(2)}) async-start(), calls=%async_computation.1 | async-start | bytes 11943936 | tf_op jit(solution)/shard_map/all_gather | solution.py:640
  11.7 6.8 %copy-start.9 = (bf16[384,768]{1,0:T(8,128)(2,1)S(1)}, bf16[384,768]{1,0:T(8,128)(2,1)}, u32[]{:S(2)}) copy-start(bf16[384,768]{1,0:T(8,128)(2,1)} %param.40) | copy-start | bytes 1769476
  11.7 14.8 %collective-permute-start = (bf16[304,768]{1,0:T(8,128)(2,1)}, bf16[304,768]{1,0:T(8,128)(2,1)S(1)}, u32[]{:S(2)}, u32[]{:S(2)}) collective-permute-start(bf16[304,768]{1,0:T(8,128)(2,1)} %pack_share.1.refs_0_), channel_id=1, source_target_pairs={{0,6},{1,7},{2,4},{3,5},{4,2},{5,3},{6,0},{7,1},{8,14},{9,15},{10,... | collective-permute-start | bytes 1400840 | tf_op jit(solution)/shard_map/ppermute | solution.py:593
  16.6 10.1 %copy-start.2 = (bf16[304,768]{1,0:T(8,128)(2,1)S(1)}, bf16[304,768]{1,0:T(8,128)(2,1)}, u32[]{:S(2)}) copy-start(bf16[304,768]{1,0:T(8,128)(2,1)} %pack_share.1.refs_0_) | copy-start | bytes 1400836
  18.6 8.0 %copy-start.7 = (bf16[864,768]{1,0:T(8,128)(2,1)}, bf16[864,768]{1,0:T(8,128)(2,1)S(1)}, u32[]{:S(2)}) copy-start(bf16[864,768]{1,0:T(8,128)(2,1)S(1)} %constant_dynamic-update-slice_fusion) | copy-start | bytes 3981316
  26.5 17.4 %copy-start.3 = (bf16[304,768]{1,0:T(8,128)(2,1)}, bf16[304,768]{1,0:T(8,128)(2,1)S(1)}, u32[]{:S(2)}) copy-start(bf16[304,768]{1,0:T(8,128)(2,1)S(1)} %collective-permute-done.refs_3_) | copy-start | bytes 1400836
  26.6 17.5 %copy-start.10 = (s32[2048]{0:T(1024)S(1)}, s32[2048]{0:T(1024)}, u32[]{:S(2)}) copy-start(s32[2048]{0:T(1024)} %param.27) | copy-start | bytes 24580
  26.6 20.4 %copy-start.12 = (s32[2048]{0:T(1024)S(1)}, s32[2048]{0:T(1024)}, u32[]{:S(2)}) copy-start(s32[2048]{0:T(1024)} %param.24) | copy-start | bytes 24580
  26.6 373.8 %reduce-scatter.2.cloned.1.call-start = ((), (), s32[]{:S(2)}) async-start(), calls=%async_computation.2 | async-start | bytes 11943936 | tf_op jit(solution)/shard_map/reduce_scatter | solution.py:647
  26.7 11.9 %collective-permute-start.2 = (bf16[304,768]{1,0:T(8,128)(2,1)S(1)}, bf16[304,768]{1,0:T(8,128)(2,1)S(1)}, u32[]{:S(2)}, u32[]{:S(2)}) collective-permute-start(bf16[304,768]{1,0:T(8,128)(2,1)S(1)} %copy-done.2), channel_id=1, source_target_pairs={{0,4},{1,5},{2,6},{3,7},{4,0},{5,1},{6,2},{7,3},{8,12},{9,13},{10,... | collective-permute-start | bytes 1400840 | tf_op jit(solution)/shard_map/ppermute | solution.py:593
  28.4 14.1 %collective-permute-start.1 = (bf16[304,768]{1,0:T(8,128)(2,1)S(1)}, bf16[304,768]{1,0:T(8,128)(2,1)S(1)}, u32[]{:S(2)}, u32[]{:S(2)}) collective-permute-start(bf16[304,768]{1,0:T(8,128)(2,1)S(1)} %copy-done.2), channel_id=1, source_target_pairs={{0,2},{1,3},{2,0},{3,1},{4,6},{5,7},{6,4},{7,5},{8,10},{9,11},{10,... | collective-permute-start | bytes 1400840 | tf_op jit(solution)/shard_map/ppermute | solution.py:593
  38.6 5.4 %copy-start.4 = (bf16[304,768]{1,0:T(8,128)(2,1)}, bf16[304,768]{1,0:T(8,128)(2,1)S(1)}, u32[]{:S(2)}) copy-start(bf16[304,768]{1,0:T(8,128)(2,1)S(1)} %collective-permute-done.2.refs_2_) | copy-start | bytes 1400836
  42.6 1.4 copy-start.5
  44.0 5.4 %collective-permute-start.3 = (bf16[1216,768]{1,0:T(8,128)(2,1)}, bf16[1216,768]{1,0:T(8,128)(2,1)S(1)}, u32[]{:S(2)}, u32[]{:S(2)}) collective-permute-start(bf16[1216,768]{1,0:T(8,128)(2,1)} %pad_maximum_fusion), channel_id=1, source_target_pairs={{0,1},{1,0},{2,3},{3,2},{4,5},{5,4},{6,7},{7,6},{8,9},{9,8},{10,11... | collective-permute-start | bytes 5603336 | tf_op jit(solution)/shard_map/ppermute | solution.py:593
  49.4 1.3 copy-start
  53.0 21.4 %copy-start.11 = (f32[1,768]{1,0:T(1,128)}, f32[1,768]{1,0:T(1,128)S(1)}, u32[]{:S(2)}) copy-start(f32[1,768]{1,0:T(1,128)S(1)} %tile.24.gq_ref) | copy-start | bytes 9220
  227.9 1.5 copy-start.13
  227.9 1.5 copy-start.14
  228.0 259.9 %all-reduce.2.cloned.1.call-start = ((), (), s32[]{:S(2)}) async-start(), calls=%async_computation.3 | async-start | bytes 2654208 | tf_op jit(solution)/shard_map/psum | solution.py:648
  334.4 25.1 %copy-start.6 = (bf16[1216,768]{1,0:T(8,128)(2,1)S(1)}, bf16[1216,768]{1,0:T(8,128)(2,1)}, u32[]{:S(2)}) copy-start(bf16[1216,768]{1,0:T(8,128)(2,1)} %get-tuple-element.93) | copy-start | bytes 5603332
  334.4 10.1 %collective-permute-start.4 = (bf16[1216,768]{1,0:T(8,128)(2,1)}, bf16[1216,768]{1,0:T(8,128)(2,1)S(1)}, u32[]{:S(2)}, u32[]{:S(2)}) collective-permute-start(bf16[1216,768]{1,0:T(8,128)(2,1)} %get-tuple-element.94), channel_id=1, source_target_pairs={{0,1},{1,0},{2,3},{3,2},{4,5},{5,4},{6,7},{7,6},{8,9},{9,8},{10,11... | collective-permute-start | bytes 5603336 | tf_op jit(solution)/shard_map/ppermute | solution.py:593
  345.9 13.6 %collective-permute-start.5 = (bf16[608,768]{1,0:T(8,128)(2,1)S(1)}, bf16[608,768]{1,0:T(8,128)(2,1)S(1)}, u32[]{:S(2)}, u32[]{:S(2)}) collective-permute-start(bf16[608,768]{1,0:T(8,128)(2,1)S(1)} %add_convert_fusion), channel_id=1, source_target_pairs={{0,2},{1,5},{2,0},{3,7},{4,6},{5,1},{6,4},{7,3},{8,10},{9,13},{10,... | collective-permute-start | bytes 2801672 | tf_op jit(solution)/shard_map/ppermute | solution.py:597
  359.7 28.1 %collective-permute-start.6 = (bf16[304,768]{1,0:T(8,128)(2,1)S(1)}, bf16[304,768]{1,0:T(8,128)(2,1)S(1)}, u32[]{:S(2)}, u32[]{:S(2)}) collective-permute-start(bf16[304,768]{1,0:T(8,128)(2,1)S(1)} %add_convert_fusion.4), channel_id=1, source_target_pairs={{0,4},{1,3},{2,6},{3,1},{4,0},{5,7},{6,2},{7,5},{8,12},{9,11},{10,... | collective-permute-start | bytes 1400840 | tf_op jit(solution)/shard_map/ppermute | solution.py:597
  388.1 10.1 %collective-permute-start.7 = (bf16[304,768]{1,0:T(8,128)(2,1)S(1)}, bf16[304,768]{1,0:T(8,128)(2,1)S(1)}, u32[]{:S(2)}, u32[]{:S(2)}) collective-permute-start(bf16[304,768]{1,0:T(8,128)(2,1)S(1)} %add_convert_fusion.3), channel_id=1, source_target_pairs={{0,8},{24,16},{1,9},{25,17},{2,10},{26,18},{3,11},{27,19},{4,12},{... | collective-permute-start | bytes 1400840 | tf_op jit(solution)/shard_map/ppermute | solution.py:601
  398.3 0.7 collective-permute-start.8
  399.1 42.3 %collective-permute-start.9 = (bf16[304,768]{1,0:T(8,128)(2,1)S(1)}, bf16[304,768]{1,0:T(8,128)(2,1)S(1)}, u32[]{:S(2)}, u32[]{:S(2)}) collective-permute-start(bf16[304,768]{1,0:T(8,128)(2,1)S(1)} %add_convert_fusion.1), channel_id=1, source_target_pairs={{8,0},{16,24},{9,1},{17,25},{10,2},{18,26},{11,3},{19,27},{12,4},{... | collective-permute-start | bytes 1400840 | tf_op jit(solution)/shard_map/ppermute | solution.py:601
  489.9 1.7 copy-start.1
Sparse Core Ops, SparseCore 0:
  26.7 65.6 all-gather.1
  228.1 96.7 reduce-scatter.1
  400.6 87.2 all-reduce.1
